TPU v7x, 32 devices: a whole 2x2x4 slice. The times are simulated.
32 devices in a mesh: batch: 8 (over z, x), head: 4 (over y, core).
Axes of the slice: x: 2, y: 2, z: 4, core: 2. Of those that a mesh axis runs over, the one named last changes fastest.
Arguments:
- tokens: bfloat16 [16384, 768], P(('batch', 'head')), may hold values from -6 to 6
- cotangent: bfloat16 [16384, 768], P(('batch', 'head')), may hold values from -6 to 6
- lengths: int32 [8, 3], P('batch'), may hold values from 1 to 1024, 2048 in all within a row
- input_weight: float32 [2304, 768], P(('batch', 'head')), may hold values from -0.21875 to 0.21875
- output_weight: float32 [768, 768], P(('batch', 'head')), may hold values from -0.875 to 0.875
- expand_weight: float32 [3072, 768], P(('batch', 'head')), may hold values from -0.21875 to 0.21875
- contract_weight: float32 [768, 3072], P(('batch', 'head')), may hold values from -0.109375 to 0.109375
- vector_params: float32 [9216], replicated, may hold values from -0.8 to 1.6, as said below
- input_first: float32 [2304, 768], P(('batch', 'head')), may hold values from -0.005859375 to 0.005859375
- input_second: float32 [2304, 768], P(('batch', 'head')), may hold values from 1.4128508e-07 to 5.6514034e-07
- output_first: float32 [768, 768], P(('batch', 'head')), may hold values from -0.005859375 to 0.005859375
- output_second: float32 [768, 768], P(('batch', 'head')), may hold values from 1.4128508e-07 to 5.6514034e-07
- expand_first: float32 [3072, 768], P(('batch', 'head')), may hold values from -0.005859375 to 0.005859375
- expand_second: float32 [3072, 768], P(('batch', 'head')), may hold values from 1.4128508e-07 to 5.6514034e-07
- contract_first: float32 [768, 3072], P(('batch', 'head')), may hold values from -0.005859375 to 0.005859375
- contract_second: float32 [768, 3072], P(('batch', 'head')), may hold values from 1.4128508e-07 to 5.6514034e-07
- vector_first: float32 [9216], replicated, may hold values from -0.0234375 to 0.0234375
- vector_second: float32 [9216], replicated, may hold values from 2.2605614e-06 to 9.042245e-06
Outputs:
- block_out: bfloat16 [16384, 768], P(('batch', 'head'))
- input_grad: bfloat16 [16384, 768], P(('batch', 'head'))
- grad_norm: float32 [], replicated
- matrix_norms: float32 [8], replicated
- input_first_new: float32 [2304, 768], P(('batch', 'head'))
- input_second_new: float32 [2304, 768], P(('batch', 'head'))
- input_weight_new: float32 [2304, 768], P(('batch', 'head'))
- input_weight_low: bfloat16 [2304, 768], P(('batch', 'head'))
- output_first_new: float32 [768, 768], P(('batch', 'head'))
- output_second_new: float32 [768, 768], P(('batch', 'head'))
- output_weight_new: float32 [768, 768], P(('batch', 'head'))
- output_weight_low: bfloat16 [768, 768], P(('batch', 'head'))
- expand_first_new: float32 [3072, 768], P(('batch', 'head'))
- expand_second_new: float32 [3072, 768], P(('batch', 'head'))
- expand_weight_new: float32 [3072, 768], P(('batch', 'head'))
- expand_weight_low: bfloat16 [3072, 768], P(('batch', 'head'))
- contract_first_new: float32 [768, 3072], P(('batch', 'head'))
- contract_second_new: float32 [768, 3072], P(('batch', 'head'))
- contract_weight_new: float32 [768, 3072], P(('batch', 'head'))
- contract_weight_low: bfloat16 [768, 3072], P(('batch', 'head'))
- vector_first_new: float32 [9216], replicated
- vector_second_new: float32 [9216], replicated
- vector_params_new: float32 [9216], replicated
Inputs may be any that keep to these rules, and one draw needn't show every extreme that they name: Each row holds 3 lengths summing to 2048; the longest in every row is exactly half of 2048. `vector_params`: entries 0 to 767 and 1536 to 2303 are norm gains near 1; the rest are shifts and biases.
All inputs are finite; a program needn't handle non-finite values.
Results may differ from a plain program's by a relative error of at most 0.012.
Values may be sent and summed in bfloat16 or wider, within the bound.
No kernel may reach another device: no remote copies, remote signals or barrier semaphores. Data moves between devices by JAX's collectives and lax.ppermute only.
A program may use at most 192 MiB of HBM per device.

v0:
```python
from functools import partial
import jax
import jax.numpy as jnp
from jax import lax
from jax.experimental import pallas as pl
from jax.experimental.pallas import tpu as pltpu
from jax.sharding import PartitionSpec as P

D = 768
HD = 64
FF = 3072
STEP = 5
NORM_EPS = 1e-05
ADAM_EPS = 1e-06
DECAY_RATE = 0.01
MATRIX_RATE = 0.5
VECTOR_RATE = 0.1
ROOT_TWO_OVER_PI = (2.0 / 3.141592653589793) ** 0.5
BLOCK = 256
LANES = 256
NT = (((1,), (1,)), ((), ()))
NN = (((1,), (0,)), ((), ()))
F32 = jnp.float32
BF16 = jnp.bfloat16


def mm(a, b, dims):
    return lax.dot_general(a, b, dims, preferred_element_type=F32)


def block_start(index, per_piece, me):
    piece = index // per_piece
    return pl.multiple_of(((piece ^ me) * per_piece + index % per_piece) * BLOCK, BLOCK)


def starts_of(scalars, docs, positions):
    first = jnp.zeros_like(positions)
    for doc in range(docs - 1):
        end = scalars[ENDS + doc]
        first = jnp.where(positions >= end, end, first)
    return first


def first_block(scalars, docs, index):
    position = index * BLOCK
    first = jnp.int32(0)
    for doc in range(docs - 1):
        end = scalars[ENDS + doc]
        first = jnp.where(position >= end, end, first)
    return first // BLOCK


def head_lanes(block, heads):
    if heads == 1:
        return [block]
    lane = lax.broadcasted_iota(jnp.int32, block.shape, 1) // HD
    return [jnp.where(lane == j, block, jnp.zeros_like(block)) for j in range(heads)]


def allowed_mask(index, key_block, doc_first):
    key = key_block * BLOCK + lax.broadcasted_iota(jnp.int32, (BLOCK, BLOCK), 0)
    if index is None:
        return key >= doc_first
    query = index * BLOCK + lax.broadcasted_iota(jnp.int32, (1, BLOCK), 1)
    return (key <= query) & (key >= doc_first)


def over_keys(first, last, key_step, state):
    pairs = (last - first) // 2

    def two(p, state):
        return key_step(first + 2 * p + 1, key_step(first + 2 * p, state))

    state = lax.fori_loop(0, pairs, two, state)
    return lax.fori_loop(first + 2 * pairs, last, key_step, state)


def group_lanes(group, kind):
    start = kind * LANES + group * HEAD_LANES
    return slice(start, start + HEAD_LANES)


def forward_body(heads, docs, per_piece, span, final, scalars, qkv, *refs):
    if span[0] > 0:
        refs = refs[2:]
    out_t, log_out, *ends, values_t = refs
    me = scalars[HERE]
    width = heads * HD

    def transpose_values(i, carry):
        v = qkv[pl.ds(block_start(i, per_piece, me), BLOCK), group_lanes(0, 2)]
        values_t[:, pl.ds(pl.multiple_of(i * BLOCK, BLOCK), BLOCK)] = v.T[:width]
        return carry

    lax.fori_loop(0, span[1], transpose_values, 0)

    def query_block(i, carry):
        row = block_start(i, per_piece, me)
        q_heads = head_lanes(qkv[pl.ds(row, BLOCK), group_lanes(0, 0)] * BF16(HD ** -0.5), heads)
        positions = i * BLOCK + lax.broadcasted_iota(jnp.int32, (1, BLOCK), 1)
        doc_first = starts_of(scalars, docs, positions)

        def key_step(kb, state, query=None):
            allowed = allowed_mask(query, kb, doc_first)
            k = qkv[pl.ds(block_start(kb, per_piece, me), BLOCK), group_lanes(0, 1)]
            column = pl.ds(pl.multiple_of(kb * BLOCK, BLOCK), BLOCK)
            new = []
            for j in range(heads):
                top, total, acc = state[j]
                s = jnp.where(allowed, mm(k, q_heads[j], NT), -1e30)
                top_new = jnp.maximum(top, jnp.max(s, axis=0, keepdims=True))
                p = jnp.exp(s - top_new)
                fade = jnp.exp(top - top_new)
                total = total * fade + jnp.sum(p, axis=0, keepdims=True)
                v_t = values_t[j * HD : (j + 1) * HD, column]
                acc = acc * fade + mm(v_t, p.astype(BF16), NN)
                new.append((top_new, total, acc))
            return tuple(new)

        init = tuple(
            (jnp.full((1, BLOCK), -1e30, F32), jnp.zeros((1, BLOCK), F32), jnp.zeros((HD, BLOCK), F32))
            for _ in range(heads)
        )
        state = key_step(i, init, i)
        state = lax.fori_loop(first_block(scalars, docs, i), i, key_step, state)
        column = pl.ds(row, BLOCK)
        for j in range(heads):
            top, total, acc = state[j]
            out_t[j * HD : (j + 1) * HD, column] = (acc / total).astype(BF16)
            log_out[j : j + 1, pl.ds(pl.multiple_of(i * BLOCK, BLOCK), BLOCK)] = top + jnp.log(total)
        return carry

    if span[0] == 0:
        log_out[...] = jnp.zeros_like(log_out)
    lax.fori_loop(span[0], span[1], query_block, 0)
    if final:
        half = out_t.shape[1] // 2
        ends[0][...] = out_t[:, :half]
        ends[1][...] = out_t[:, half:]


def attention_forward(scalars, qkv, heads, docs, piece, span, before=(), markers=()):
    rows = qkv.shape[0]
    width = heads * HD
    final = span[1] == rows // BLOCK
    inputs = [scalars, qkv, *before]
    outs = [shape((width, rows), BF16), shape((8, rows), F32)]
    return call(
        partial(forward_body, heads, docs, piece // BLOCK, span, final),
        inputs,
        outs + [shape((width, rows // 2), BF16)] * (2 * final),
        [pltpu.VMEM((width, rows), BF16)],
        14,
        "attention_forward",
        markers=markers,
        aliases={len(inputs) - 2 + i: i for i in range(2)} if before else {},
    )


def backward_body(
    heads, docs, per_piece, span, final, scalars, qkv, out_keep, out_send, grad_keep, grad_recv, logs, *refs
):
    if span[0] > 0:
        refs = refs[3:]
    grads, d_keys, d_values, sums, keys_t, out_t, grad_t = refs
    me = scalars[HERE]
    width = heads * HD
    scale = HD ** -0.5
    half = out_keep.shape[1]
    out_t[:, :half] = out_keep[...]
    out_t[:, half:] = out_send[...]
    grad_t[:, :half] = grad_keep[...]
    grad_t[:, half:] = grad_recv[...]
    if span[0] == 0:
        d_keys[...] = jnp.zeros_like(d_keys)
        d_values[...] = jnp.zeros_like(d_values)

    def transpose_keys(i, carry):
        k = qkv[pl.ds(block_start(i, per_piece, me), BLOCK), group_lanes(0, 1)]
        keys_t[:, pl.ds(pl.multiple_of(i * BLOCK, BLOCK), BLOCK)] = k.T[:width]
        return carry

    lax.fori_loop(0, span[1], transpose_keys, 0)

    def padded(rows, kind):
        return jnp.concatenate([rows, jnp.zeros((LANES - width, BLOCK), kind)], axis=0)

    def query_block(i, carry):
        row = block_start(i, per_piece, me)
        q_heads = head_lanes(qkv[pl.ds(row, BLOCK), group_lanes(0, 0)] * BF16(scale), heads)
        o_t = out_t[:, pl.ds(row, BLOCK)]
        g_t = grad_t[:, pl.ds(row, BLOCK)]
        product = o_t.astype(F32) * g_t.astype(F32)
        deltas = [jnp.sum(product[j * HD : (j + 1) * HD], axis=0, keepdims=True) for j in range(heads)]
        g_heads = head_lanes(padded(g_t, BF16).T, heads)
        natural = pl.ds(pl.multiple_of(i * BLOCK, BLOCK), BLOCK)
        log_rows = [logs[j : j + 1, natural] for j in range(heads)]
        positions = i * BLOCK + lax.broadcasted_iota(jnp.int32, (1, BLOCK), 1)
        doc_first = starts_of(scalars, docs, positions)

        def key_step(kb, d_q, query=None):
            allowed = allowed_mask(query, kb, doc_first)
            key_row = pl.ds(block_start(kb, per_piece, me), BLOCK)
            k = qkv[key_row, group_lanes(0, 1)]
            v = qkv[key_row, group_lanes(0, 2)]
            column = pl.ds(pl.multiple_of(kb * BLOCK, BLOCK), BLOCK)
            d_k = d_keys[key_row, :]
            d_v = d_values[key_row, :]
            new = []
            for j in range(heads):
                s = jnp.where(allowed, mm(k, q_heads[j], NT), -1e30)
                p = jnp.exp(s - log_rows[j])
                d_v = d_v + mm(p.astype(BF16), g_heads[j], NN)
                d_p = mm(v, g_heads[j], NT)
                d_s = (p * (d_p - deltas[j])).astype(BF16)
                d_k = d_k + mm(d_s, q_heads[j], NN)
                new.append(d_q[j] + mm(keys_t[j * HD : (j + 1) * HD, column], d_s, NN))
            d_keys[key_row, :] = d_k
            d_values[key_row, :] = d_v
            return tuple(new)

        d_q = key_step(i, tuple(jnp.zeros((HD, BLOCK), F32) for _ in range(heads)), i)
        d_q = over_keys(first_block(scalars, docs, i), i, key_step, d_q)
        stacked = padded(jnp.concatenate(d_q, axis=0), F32) * scale
        grads[pl.ds(row, BLOCK), 0:LANES] = stacked.T.astype(BF16)
        return carry

    lax.fori_loop(span[0], span[1], query_block, 0)
    sums[...] = jnp.zeros_like(sums)
    if final:
        grads[:, LANES : 2 * LANES] = d_keys[...].astype(BF16)
        grads[:, 2 * LANES : 3 * LANES] = d_values[...].astype(BF16)
        for line, kind in enumerate((0, 2)):
            columns = grads[:, kind * LANES : (kind + 1) * LANES].astype(F32)
            sums[line : line + 1, :] = jnp.sum(columns, axis=0, keepdims=True)


def attention_backward(scalars, qkv, outs, grads, logs, heads, docs, piece, span, before=(), markers=()):
    rows = qkv.shape[0]
    width = heads * HD
    final = span[1] == rows // BLOCK
    inputs = [scalars, qkv, *outs, *grads, logs, *before]
    return call(
        partial(backward_body, heads, docs, piece // BLOCK, span, final),
        inputs,
        [
            shape((rows, 3 * LANES), BF16),
            shape((rows, LANES), F32),
            shape((rows, LANES), F32),
            shape((8, LANES), F32),
        ],
        [pltpu.VMEM((width, rows), BF16)] * 3,
        19,
        "attention_backward",
        markers=markers,
        aliases={len(inputs) - 3 + i: i for i in range(3)} if before else {},
    )


MICROSECONDS = {
    "prepare": 2.8,
    "block_kinds": 0.5,
    "join": 1.2,
    "project": 5,
    "attention_forward": 8,
    "branch": 1.3,
    "middle_norm": 0.2,
    "rise": 0.1,
    "feed_forward": 11,
    "head_gradients": 0.2,
    "output_weight_gradient": 0.2,
    "attention_backward": 2,
    "first_norm_gradient": 0.5,
    "input_weight_gradient": 1,
    "add_arrived": 0.05,
    "middle_gradient": 0.4,
    "first_gradient": 2.5,
    "payload": 1,
    "expand_gradient": 0.4,
    "contract_gradient": 0.4,
    "moments": 2,
    "directions": 1,
    "weights": 1.5,
}
COST_SCALE = 1.0


def cost(name):
    flops = int(MICROSECONDS[name] * COST_SCALE * 1.0e9)
    return pl.CostEstimate(flops=flops, bytes_accessed=0, transcendentals=0)


VMEM = pl.BlockSpec(memory_space=pltpu.VMEM)
SMEM = pl.BlockSpec(memory_space=pltpu.SMEM)
LEFT = pl.BlockSpec(memory_space=pl.ANY)
TN = (((0,), (0,)), ((), ()))
HERE, CHIP, ROW, CORE, SIDE, PLACE = range(6)
ENDS = 6


class Places:
    def __init__(self, lengths=None):
        self.lengths = lengths

    def __getitem__(self, number):
        here, row = lax.axis_index("head"), lax.axis_index("batch")
        heads, rows = lax.axis_size("head"), lax.axis_size("batch")
        if number == HERE:
            return here
        if number == CHIP:
            return row * (heads // 2) + here // 2
        if number == ROW:
            return row
        if number == CORE:
            return here % 2
        if number == SIDE:
            return here // 2
        if number == PLACE:
            return rows * here + row
        return sum(self.lengths[0, doc] for doc in range(number - ENDS + 1))


def call(body, inputs, outputs, scratch, mib, name, markers=(), aliases={}):
    lengths, inputs = inputs[0].lengths, inputs[1:]
    lead = [] if lengths is None else [lengths]
    count = len(lead) + len(inputs)

    def whole(*refs):
        places = Places(refs[0] if lead else None)
        body(places, *refs[len(lead) : count], *refs[count + len(markers) :])

    return pl.pallas_call(
        whole,
        out_shape=tuple(outputs),
        in_specs=[SMEM] * len(lead) + [VMEM] * len(inputs) + [LEFT] * len(markers),
        out_specs=(VMEM,) * len(outputs),
        scratch_shapes=scratch,
        input_output_aliases=aliases,
        compiler_params=pltpu.CompilerParams(vmem_limit_bytes=mib * 2**20),
        cost_estimate=cost(name),
        name=name,
    )(*lead, *inputs, *markers)


def lines_row(lines, first, count):
    return jnp.concatenate([lines[pl.ds(first + i, 1), :] for i in range(count)], axis=1)


def vector_row(lines, number):
    return lines_row(lines, number * (D // 128), D // 128)


def heads_row(lines, number, here):
    width = D // lax.axis_size("head")
    row = lines_row(lines, number * (D // 128) + (width * here) // 128, LANES // 128)
    row = jnp.where((width * here) % 128 != 0, pltpu.roll(row, LANES - HD, 1), row)
    lane = lax.broadcasted_iota(jnp.int32, row.shape, 1)
    return jnp.where(lane < width, row, 0.0)


def shape(dims, kind):
    return jax.ShapeDtypeStruct(tuple(dims), kind)


def join_pairs(ins, outs, cuts):
    outs = list(outs)
    for i, cut in enumerate(cuts):
        own, arrived = ins[2 * i], ins[2 * i + 1]
        half = own.shape[0]
        if cut == 0:
            out = outs.pop(0)
            out[:half] = own[...]
            out[half:] = arrived[...]
            continue
        rows = own.shape[1] // cut
        for part in range(cut):
            out = outs.pop(0)
            out[:half] = own[:, part * rows : (part + 1) * rows]
            out[half:] = arrived[:, part * rows : (part + 1) * rows]


def join_body(cuts, scalars, *refs):
    count = 2 * len(cuts)
    join_pairs(refs[:count], refs[count:], cuts)


def join_shapes(pairs, cuts):
    shapes = []
    for (own, _), cut in zip(pairs, cuts):
        dims = (2 * own.shape[0],) + own.shape[1:]
        if cut == 0:
            shapes.append(shape(dims, own.dtype))
        else:
            shapes += [shape((dims[0], dims[1] // cut, dims[2]), own.dtype)] * cut
    return shapes


def join(scalars, pairs, cuts, markers=()):
    flat = [x for pair in pairs for x in pair]
    return call(
        partial(join_body, cuts), [scalars, *flat], join_shapes(pairs, cuts), [], 24, "join", markers=markers
    )


def prepare_body(scalars, weight_in, weight_expand, weight_out, weight_back, tokens, lines, *outs):
    blocks, (expand, mine, other, back, normed) = outs[:3], outs[3:]
    back[...] = weight_back[...].astype(BF16)
    rows = blocks[0].shape[0]
    for slot, out in enumerate(blocks):
        out[...] = weight_in[slot * rows : (slot + 1) * rows, :].astype(BF16)
    expand[...] = weight_expand[...].astype(BF16)
    quarter = D // 4
    wide = weight_out[...]
    even = jnp.concatenate([wide[:, :quarter], wide[:, 2 * quarter : 3 * quarter]], axis=1)
    odd = jnp.concatenate([wide[:, quarter : 2 * quarter], wide[:, 3 * quarter :]], axis=1)
    high = scalars[CORE] == 1
    mine[...] = jnp.where(high, odd, even).astype(BF16)
    other[...] = jnp.where(high, even, odd).astype(BF16)
    gain, shift = vector_row(lines, 0), vector_row(lines, 1)
    step = min(128, tokens.shape[0])
    for start in range(0, tokens.shape[0], step):
        unit, _ = row_norm(tokens[start : start + step, :].astype(F32))
        normed[start : start + step, :] = (unit * gain + shift).astype(BF16)


def prepare(scalars, weight_in, weight_expand, weight_out, weight_back, tokens, lines):
    rows, out_rows = weight_in.shape[0] // 3, weight_out.shape[0]
    return call(
        prepare_body,
        [scalars, weight_in, weight_expand, weight_out, weight_back, tokens, lines],
        [shape((rows, D), BF16)] * 3
        + [
            shape(weight_expand.shape, BF16),
            shape((out_rows, D // 2), BF16),
            shape((out_rows, D // 2), BF16),
            shape(weight_back.shape, BF16),
            shape(tokens.shape, BF16),
        ],
        [],
        60,
        "prepare",
    )


def kinds_body(total, scalars, first, second, third, out):
    place = scalars[PLACE]
    rows = first.shape[0]
    for slot, block in enumerate((first, second, third)):
        kind = ((slot + 3 * total - place) * total) % 3
        out[kind] = block[...]


def block_kinds(scalars, blocks, total):
    rows = blocks[0].shape[0]
    outs = [shape((3, rows, D), BF16)]
    return call(partial(kinds_body, total), [scalars, *blocks], outs, [], 8, "block_kinds")[0]


def spread(scalars, base, parts, masks, put):
    origin = scalars[base] if base is not None else 0
    for ref, own in zip(parts, masks):
        for r, mask in enumerate(own):
            put(origin ^ mask if base is not None else mask, ref[r])


def project_body(base, masks, cuts, scalars, mine, other, lines, *refs):
    parts, refs = refs[: len(masks)], refs[len(masks) :]
    pairs, refs = refs[: 2 * len(cuts)], refs[2 * len(cuts) :]
    out, weight_out, weight = refs[0], refs[1], refs[-1]
    join_pairs(pairs, refs[2:-1], cuts)
    weight[...] = jnp.zeros_like(weight)

    def put(place, chunk):
        rows = chunk.shape[0] // 3
        wide = chunk.astype(F32)
        for kind in range(3):
            start = kind * LANES + place * rows
            if base is not None:
                start = pl.multiple_of(start, 8)
            weight[pl.ds(start, rows), :] = wide[kind * rows : (kind + 1) * rows]

    spread(scalars, base, parts, masks, put)
    low = weight[...].astype(BF16)
    weight_out[...] = low
    piece = mine.shape[0] // 2
    here = scalars[HERE]
    bias = jnp.concatenate(
        [heads_row(lines, 4, here), jnp.zeros((1, LANES), F32), heads_row(lines, 5, here)], axis=1
    )
    for place, (source, lead) in enumerate(((mine, 0), (other, 0), (mine, piece), (other, piece))):
        rows = source[lead : lead + piece, :]
        out[place * piece : (place + 1) * piece, :] = (mm(rows, low, NT) + bias).astype(BF16)


def project(scalars, mine, other, lines, base, parts, masks, pairs, cuts, markers):
    rows = 2 * mine.shape[0]
    flat = [x for pair in pairs for x in pair]
    outs = [shape((rows, 3 * LANES), BF16), shape((3 * LANES, D), BF16), *join_shapes(pairs, cuts)]
    found = call(
        partial(project_body, base, masks, cuts),
        [scalars, mine, other, lines, *parts, *flat],
        outs,
        [pltpu.VMEM((3 * LANES, D), F32)],
        24,
        "project",
        markers=markers,
    )
    return found[0], found[1], found[2:]


def branch_body(base, masks, scalars, keep, across_t, *refs):
    parts, refs = refs[: len(masks)], refs[len(masks) :]
    sent_a, sent_b, kept, own_out, across_out, weight = refs
    width = own_out.shape[1]

    def put(place, chunk):
        rows = chunk.shape[0]
        start = pl.multiple_of(place * rows, 16) if base is not None else place * rows
        for group in range(2):
            weight[group, pl.ds(start, rows), :] = chunk[:, group * width : (group + 1) * width]

    spread(scalars, base, parts, masks, put)
    side = scalars[SIDE]
    own_out[...] = weight[side]
    across_out[...] = weight[1 - side]
    piece = kept.shape[0]
    def rows_of(columns):
        return mm(keep[:, columns].T, own_out[...], NT) + mm(across_t[:, columns].T, across_out[...], NT)

    half = piece // 2
    sent_a[...] = rows_of(slice(piece, piece + half)).astype(BF16)
    sent_b[...] = rows_of(slice(piece + half, 2 * piece)).astype(BF16)
    kept[...] = rows_of(slice(0, piece))


def middle_norm_body(scalars, tokens, kept, arrived_a, arrived_b, lines, middle, normed_a, normed_b):
    bias, gain, shift = vector_row(lines, 6), vector_row(lines, 2), vector_row(lines, 3)
    half = normed_a.shape[0]
    step = min(128, half)
    for lead, arrived, normed in ((0, arrived_a, normed_a), (half, arrived_b, normed_b)):
        for start in range(0, half, step):
            rows = slice(lead + start, lead + start + step)
            values = tokens[rows, :].astype(F32) + kept[rows, :]
            values = values + arrived[start : start + step, :].astype(F32) + bias
            middle[rows, :] = values
            unit, _ = row_norm(values)
            normed[start : start + step, :] = (unit * gain + shift).astype(BF16)


def middle_norm(scalars, tokens, kept, arrived, lines, markers):
    piece = tokens.shape[0]
    return call(
        middle_norm_body,
        [scalars, tokens, kept, *arrived, lines],
        [shape((piece, D), F32), shape((piece // 2, D), BF16), shape((piece // 2, D), BF16)],
        [],
        16,
        "middle_norm",
        markers,
    )


def branch(scalars, keep, across_t, base, parts, masks, markers):
    width, rows = keep.shape
    piece = rows // 2
    return call(
        partial(branch_body, base, masks),
        [scalars, keep, across_t, *parts],
        [shape((piece // 2, D), BF16)] * 2
        + [shape((piece, D), F32), shape((D, width), BF16), shape((D, width), BF16)],
        [pltpu.VMEM((2, D, width), BF16)],
        24,
        "branch",
        markers=markers,
    )


MLP_ROWS = 256
MLP_LANES = 512


def rise_body(bases, masks, scalars, own_a, own_b, other_a, other_b, grad_own, grad_other, lines, *refs):
    count = sum(map(len, masks))
    parts, (activated, slopes, expand, pair, grad_pair) = refs[:count], refs[count:]
    half = expand.shape[0]
    piece = grad_own.shape[0]
    for lead, rows in enumerate((own_a, own_b, other_a, other_b)):
        pair[lead * (piece // 2) : (lead + 1) * (piece // 2), :] = rows[...]
    grad_pair[:piece, :] = grad_own[...]
    grad_pair[piece:, :] = grad_other[...]
    bias = lines_row(lines, 8 * (D // 128) + scalars[CORE] * (half // 128), half // 128)

    def put_expand(index):
        def put(place, chunk):
            rows = chunk.shape[0]
            start = place * 2 * rows + index * rows
            if bases[index] is not None:
                start = pl.multiple_of(start, 16)
            expand[pl.ds(start, rows), :] = chunk

        return put

    taken = 0
    for index, own_masks in enumerate(masks):
        spread(scalars, bases[index], parts[taken : taken + len(own_masks)], own_masks, put_expand(index))
        taken += len(own_masks)
    step = min(MLP_ROWS, piece)

    def block(i, carry):
        rows = pl.ds(pl.multiple_of(i * step, step), step)
        normed = pair[rows, :]
        for lanes in range(0, half, MLP_LANES):
            span = slice(lanes, lanes + MLP_LANES)
            expanded = mm(normed, expand[span, :], NT) + bias[:, span]
            squared = expanded * expanded
            bent = jnp.tanh(ROOT_TWO_OVER_PI * (expanded + 0.044715 * (expanded * squared)))
            rise = 0.5 * (1.0 + bent)
            activated[rows, span] = (expanded * rise).astype(BF16)
            slopes[rows, span] = rise + (0.5 * ROOT_TWO_OVER_PI) * expanded * (1.0 - bent * bent) * (
                1.0 + (3.0 * 0.044715) * squared
            )
        return carry

    lax.fori_loop(0, 2 * piece // step, block, 0)


def rise(scalars, normed, grads, lines, bases, parts, masks):
    piece = grads[0].shape[0]
    half = FF // 2
    flat = [x for group in parts for x in group]
    return call(
        partial(rise_body, bases, masks),
        [scalars, *normed, *grads, lines, *flat],
        [
            shape((2 * piece, half), BF16),
            shape((2 * piece, half), F32),
            shape((half, D), BF16),
            shape((2 * piece, D), BF16),
            shape((2 * piece, D), BF16),
        ],
        [],
        14,
        "rise",
    )


def feed_body(base, masks, scalars, activated, slopes, expand, grad_pair, *refs):
    parts, refs = refs[: len(masks)], refs[len(masks) :]
    grad_hidden, normed_sent, normed_kept, out_sent, out_kept, sums, contract = refs
    half = expand.shape[0]
    piece = normed_kept.shape[0]

    def put_contract(place, chunk):
        rows = chunk.shape[0]
        start = pl.multiple_of(place * rows, 16) if base is not None else place * rows
        contract[pl.ds(start, rows), :] = chunk

    spread(scalars, base, parts, masks, put_contract)
    sums[...] = jnp.zeros_like(sums)
    step = min(MLP_ROWS, piece)

    def block(start, lead, normed_out, contract_out):
        rows = pl.ds(start, step)
        target = pl.ds(pl.multiple_of(lead + start, step), step)
        grad = grad_pair[target, :]
        back = jnp.zeros((step, D), F32)
        result = jnp.zeros((step, D), F32)
        for lanes in range(0, half, MLP_LANES):
            span = slice(lanes, lanes + MLP_LANES)
            hidden = (mm(grad, contract[:, span], NN) * slopes[target, span]).astype(BF16)
            grad_hidden[target, span] = hidden
            sums[0:1, span] += jnp.sum(hidden.astype(F32), axis=0, keepdims=True)
            back = back + mm(hidden, expand[span, :], NN)
            result = result + mm(activated[target, span], contract[:, span], NT)
        normed_out[rows, :] = back.astype(normed_out.dtype)
        contract_out[rows, :] = result.astype(contract_out.dtype)

    def own_block(i, carry):
        block(pl.multiple_of(i * step, step), 0, normed_kept, out_kept)
        return carry

    def other_block(i, carry):
        block(pl.multiple_of(i * step, step), piece, normed_sent, out_sent)
        return carry

    lax.fori_loop(0, piece // step, other_block, 0)
    lax.fori_loop(0, piece // step, own_block, 0)


def feed_forward(scalars, activated, slopes, expand, grad_pair, base, parts, masks):
    half = expand.shape[0]
    piece = grad_pair.shape[0] // 2
    return call(
        partial(feed_body, base, masks),
        [scalars, activated, slopes, expand, grad_pair, *parts],
        [
            shape((2 * piece, half), BF16),
            shape((piece, D), BF16),
            shape((piece, D), F32),
            shape((piece, D), BF16),
            shape((piece, D), F32),
            shape((8, half), F32),
        ],
        [pltpu.VMEM((D, half), BF16)],
        18,
        "feed_forward",
    )


def head_grads_body(scalars, own, other, weight_own, weight_across, keep, sent):
    piece = own.shape[0]
    for matrix, out in ((weight_across, sent), (weight_own, keep)):
        for place, rows in enumerate((own, other)):
            features = mm(rows[...], matrix[...], NN).T.astype(BF16)
            out[:, place * piece : (place + 1) * piece] = features


def head_grads(scalars, grads, weight_own, weight_across, markers):
    piece = grads[0].shape[0]
    outs = [shape((weight_own.shape[1], 2 * piece), BF16)] * 2
    return call(head_grads_body, [scalars, *grads, weight_own, weight_across], outs, [], 16, "head_gradients", markers)


def split_rows(total, plan, scalars, sent, kept):
    which, shift, size = plan
    bit = (scalars[which] >> shift) & 1
    rows = sent.shape[1]

    def one(m, carry):
        base = (m // size) * 2 * size + m % size
        for out, chosen in ((sent, 1 - bit), (kept, bit)):
            start = pl.multiple_of((base + chosen * size) * rows, 8)
            out[m] = total[pl.ds(start, rows), :].astype(out.dtype)
        return carry

    lax.fori_loop(0, sent.shape[0], one, 0)


def split_shapes(chips, rows, columns):
    dims = (chips // 2, rows, columns)
    return [shape(dims, BF16), shape(dims, F32)]


def output_weight_body(plan, scalars, own, other, keep, across_t, *refs):
    *outs, stacked, total = refs
    side = scalars[SIDE]
    piece = own.shape[0]
    width = keep.shape[0]
    for place, features in ((side, keep), (1 - side, across_t)):
        product = mm(features[:, :piece], own[...], NN) + mm(features[:, piece:], other[...], NN)
        stacked[pl.ds(pl.multiple_of(place * width, 8), width), :] = product
    total[...] = stacked[...].T
    if plan is None:
        outs[0][...] = total[...].astype(BF16)
    else:
        split_rows(total, plan, scalars, *outs)


def output_weight_grad(scalars, grads, keep, across_t, plan, chips, markers):
    width = keep.shape[0]
    outs = [shape((D, 2 * width), BF16)] if plan is None else split_shapes(chips, D // chips, 2 * width)
    return call(
        partial(output_weight_body, plan),
        [scalars, *grads, keep, across_t],
        outs,
        [pltpu.VMEM((2 * width, D), F32), pltpu.VMEM((D, 2 * width), F32)],
        16,
        "output_weight_gradient",
        markers=markers,
    )


def product_body(plan, lanes, scalars, left, right, sent, kept, total):
    for start in range(0, left.shape[1], lanes):
        block = left[:, start : start + lanes].T
        for column in range(0, right.shape[1], D):
            columns = slice(column, column + D)
            total[start : start + lanes, columns] = mm(block, right[:, columns], NN)
    split_rows(total, plan, scalars, sent, kept)


def product_grad(scalars, left, right, plan, chips, name, markers=()):
    rows, columns = left.shape[1], right.shape[1]
    return call(
        partial(product_body, plan, 256),
        [scalars, left, right],
        split_shapes(chips, rows // chips, columns),
        [pltpu.VMEM((rows, columns), F32)],
        24,
        name,
        markers=markers,
    )


def input_weight_body(aligned, rows_of_devices, scalars, grads, mine, other, *refs):
    total = refs[-1]
    piece = mine.shape[0] // 2
    step = min(MLP_ROWS, piece)
    total[...] = jnp.zeros_like(total)
    for place, (source, lead) in enumerate(((mine, 0), (other, 0), (mine, piece), (other, piece))):
        for start in range(0, piece, step):
            rows = grads[place * piece + start : place * piece + start + step, :]
            total[...] += mm(rows.T, source[lead + start : lead + start + step, :], NN)
    if not aligned:
        natural = refs[0]
        for kind in range(3):
            natural[kind] = total[kind * LANES : kind * LANES + natural.shape[1], :]
        return
    sent, kept = refs[0], refs[1]
    rows = sent.shape[1]
    bit = (scalars[ROW] >> 1) & 1
    count = rows_of_devices // 2
    for kind in range(3):
        for e in range(count):
            for out, chosen in ((sent, 1 - bit), (kept, bit)):
                start = kind * LANES + ((e // 2) * 4 + e % 2 + 2 * chosen) * rows
                out[kind * count + e] = total[pl.ds(pl.multiple_of(start, 8), rows), :].astype(out.dtype)


def input_weight_grad(scalars, grads, mine, other, rows_of_devices, block):
    aligned = block % 8 == 0
    part = (3 * rows_of_devices // 2, block, D)
    outs = [shape(part, BF16), shape(part, F32)]
    if not aligned:
        outs = [shape((3, block * rows_of_devices, D), F32)]
    return call(
        partial(input_weight_body, aligned, rows_of_devices),
        [scalars, grads, mine, other],
        outs,
        [pltpu.VMEM((3 * LANES, D), F32)],
        16,
        "input_weight_gradient",
    )


def first_grads_body(places, scalars, grads, weight, *refs):
    *far, kept = refs
    piece = kept.shape[0]
    half = piece // 2
    halves = len(far) == 2
    if halves:
        outs = ((0, far[0]), (half, far[1]))
    else:
        far_kept, arrived_a, arrived_b, reduced, whole = far
        outs = ((0, whole),)
        for lead, arrived in ((0, arrived_a), (half, arrived_b)):
            rows = slice(lead, lead + half)
            reduced[rows, :] = (far_kept[rows, :] + arrived[...].astype(F32)).astype(BF16)
    sent, stay = places
    for lead, out in outs:
        rows = grads[sent * piece + lead : sent * piece + lead + out.shape[0], :]
        out[...] = mm(rows, weight[...], NN).astype(BF16)
    kept[...] = mm(grads[stay * piece : (stay + 1) * piece, :], weight[...], NN)


def first_grads(scalars, grads, weight, places, far=(), markers=()):
    piece = grads.shape[0] // 4
    outs = [shape((piece, D), BF16)] * 2 if far else [shape((piece // 2, D), BF16)] * 2
    return call(
        partial(first_grads_body, places),
        [scalars, grads, weight, *far],
        outs + [shape((piece, D), F32)],
        [],
        16,
        "first_norm_gradient",
        markers=markers,
    )


def payload_body(hidden_rows, scalars, inputs, expand, contract, first, middle, heads, hidden, out):
    six = D // 128
    out[...] = jnp.zeros_like(out)
    out[: 2 * six, :] = first[: 2 * six, :]
    out[2 * six : 4 * six, :] = middle[: 2 * six, :]
    out[6 * six : 8 * six, :] = middle[2 * six : 4 * six, :]
    here = scalars[HERE]
    for line in range(2):
        row = heads[line : line + 1, :]
        row = jnp.where(here % 2 == 1, pltpu.roll(row, HD, 1), row)
        start = (4 + line) * six + (3 * here) // 2
        for part in range(2):
            out[pl.ds(start + part, 1), :] = row[:, part * 128 : (part + 1) * 128]
    for part in range(hidden_rows):
        line = 8 * six + scalars[CORE] * hidden_rows + part
        out[pl.ds(line, 1), :] = hidden[0:1, part * 128 : (part + 1) * 128]
    total = jnp.zeros((1, 1), F32)
    for gradients in (inputs, expand, contract):
        for i in range(gradients.shape[0]):
            values = gradients[i]
            rows = jnp.sum(values * values, axis=1, keepdims=True)
            total += jnp.sum(rows, axis=0, keepdims=True)
    lane = lax.broadcasted_iota(jnp.int32, (1, 128), 1)
    out[VECTOR_ROWS : VECTOR_ROWS + 1, :] = jnp.where(lane == 0, total, 0.0)


def make_payload(scalars, gradients, first, middle, heads, hidden):
    return call(
        partial(payload_body, hidden.shape[1] // 128),
        [scalars, *gradients, first, middle, heads, hidden],
        [shape((VECTOR_ROWS + 8, 128), F32)],
        [],
        12,
        "payload",
    )[0]


def reduce_body(plans, scalars, *refs):
    count = 2 * sum(len(sources) for sources, _ in plans)
    ins, outs = list(refs[:count]), list(refs[count:])
    for sources, split in plans:
        terms = []
        column = 0
        for full in sources:
            kept, arrived = ins.pop(0), ins.pop(0)
            columns = slice(column, column + arrived.shape[2])
            column += arrived.shape[2]

            def total(index, kept=kept, arrived=arrived, full=full):
                source = index
                if full is not None:
                    which, shift, size = full
                    bit = (scalars[which] >> shift) & 1
                    source = (index // size) * 2 * size + bit * size + index % size
                return kept[source].astype(F32) + arrived[index].astype(F32)

            terms.append((columns, total))
        if split is None:
            out = outs.pop(0)

            def whole(m, carry, out=out, terms=terms):
                for columns, total in terms:
                    out[m, :, columns] = total(m)
                return carry

            lax.fori_loop(0, out.shape[0], whole, 0)
        else:
            which, shift, size = split
            sent_out, kept_out = outs.pop(0), outs.pop(0)

            def halves(m, carry, sent_out=sent_out, kept_out=kept_out, terms=terms):
                bit = (scalars[which] >> shift) & 1
                base = (m // size) * 2 * size + m % size
                for columns, total in terms:
                    kept_out[m, :, columns] = total(base + bit * size)
                    sent_out[m, :, columns] = total(base + (1 - bit) * size).astype(BF16)
                return carry

            lax.fori_loop(0, kept_out.shape[0], halves, 0)


HEAD_LANES = LANES


VECTOR_ROWS = (8 * D + FF) // 128


def row_norm(values):
    mean = jnp.mean(values, axis=1, keepdims=True)
    centered = values - mean
    variance = jnp.mean(centered * centered, axis=1, keepdims=True)
    inverse = lax.rsqrt(variance + NORM_EPS)
    return centered * inverse, inverse


def norm_input_gradient(upstream, values, gain):
    unit, inverse = row_norm(values)
    scaled = upstream * gain
    first = jnp.mean(scaled, axis=1, keepdims=True)
    second = jnp.mean(scaled * unit, axis=1, keepdims=True)
    return inverse * (scaled - first - unit * second), unit


def stack_rows(sums, rows):
    for place, row in enumerate(rows):
        total = jnp.sum(row, axis=0, keepdims=True)
        for part in range(D // 128):
            line = place * (D // 128) + part
            sums[line : line + 1, :] += total[:, part * 128 : (part + 1) * 128]


def middle_body(own, arrived, middle, cotangent, lines, grad_mid, grad_branch, sums):
    @pl.when(pl.program_id(0) == 0)
    def _():
        sums[...] = jnp.zeros_like(sums)

    upstream = own[...] + arrived[...].astype(F32)
    passed, unit = norm_input_gradient(upstream, middle[...], vector_row(lines, 2))
    outer = cotangent[...].astype(F32)
    total = outer + passed
    rounded = total.astype(BF16)
    grad_mid[...] = total
    grad_branch[...] = rounded
    stack_rows(sums, [upstream * unit, upstream, rounded.astype(F32), outer])


def first_body(own, arrived, across, tokens, grad_mid, lines, input_grad, sums):
    @pl.when(pl.program_id(0) == 0)
    def _():
        sums[...] = jnp.zeros_like(sums)

    upstream = own[...] + arrived[...].astype(F32) + across[...].astype(F32)
    passed, unit = norm_input_gradient(upstream, tokens[...].astype(F32), vector_row(lines, 0))
    input_grad[...] = (grad_mid[...] + passed).astype(BF16)
    stack_rows(sums, [upstream * unit, upstream])


def norm_backward(body, arrays, lines, outputs, name, markers=()):
    rows = arrays[0].shape[0]
    step = min(128, rows)
    tile = pl.BlockSpec((step, D), lambda i: (i, 0))
    row = pl.BlockSpec(lines.shape, lambda i: (0, 0))
    sums = pl.BlockSpec((24, 128), lambda i: (0, 0))
    count = len(arrays) + 1

    def whole(*refs):
        body(*refs[:count], *refs[count + len(markers) :])

    return pl.pallas_call(
        whole,
        grid=(rows // step,),
        out_shape=tuple(jax.ShapeDtypeStruct((rows, D), kind) for kind in outputs)
        + (jax.ShapeDtypeStruct((24, 128), F32),),
        in_specs=[tile] * len(arrays) + [row] + [LEFT] * len(markers),
        out_specs=tuple(tile for _ in outputs) + (sums,),
        compiler_params=pltpu.CompilerParams(vmem_limit_bytes=10 * 2**20),
        cost_estimate=cost(name),
        name=name,
    )(*arrays, lines, *markers)


def moments_body(*refs):
    payload, refs = refs[0], refs[1:]
    grads, firsts, seconds, masters = refs[0:4], refs[4:9], refs[9:14], refs[14:19]
    first_outs, second_outs, direction_outs = refs[20:25], refs[25:30], refs[30:35]
    clip = clip_of(payload)
    for place in range(5):
        gradient = grads[place][...] if place < 4 else payload[0:VECTOR_ROWS, :]
        master = masters[place][...]
        first_new, second_new, direction = direction_of(
            gradient, firsts[place][...], seconds[place][...], master, clip
        )
        first_outs[place][...] = first_new
        second_outs[place][...] = second_new
        direction_outs[place][...] = direction if place < 4 else master - VECTOR_RATE * direction


def clip_of(payload):
    vector = payload[0:VECTOR_ROWS, :]
    total = payload[VECTOR_ROWS : VECTOR_ROWS + 1, 0:1] + jnp.sum(
        jnp.sum(vector * vector, axis=1, keepdims=True), axis=0, keepdims=True
    )
    return jnp.minimum(1.0, 1.0 / jnp.sqrt(total))


def direction_of(gradient, first_old, second_old, master, clip):
    clipped = gradient * clip
    first_new = 0.5 * first_old + 0.5 * clipped
    second_new = 0.5 * second_old + 0.5 * clipped * clipped
    correction = 1.0 - 0.5**STEP
    direction = (
        first_new / correction / (jnp.sqrt(second_new / correction) + ADAM_EPS) + DECAY_RATE * master
    )
    return first_new, second_new, direction


def directions_body(*refs):
    payload, squares, refs = refs[0], refs[-1], refs[1:-1]
    grads, firsts, seconds, masters = refs[0:4], refs[4:8], refs[8:12], refs[12:16]
    clip = clip_of(payload)
    lane = lax.broadcasted_iota(jnp.int32, squares.shape, 1)
    row = lax.broadcasted_iota(jnp.int32, squares.shape, 0)
    found = jnp.zeros(squares.shape, F32)
    for place in range(4):
        master = masters[place][...]
        _, _, direction = direction_of(
            grads[place][...], firsts[place][...], seconds[place][...], master, clip
        )
        for offset, values in ((0, direction), (4, master)):
            square = jnp.sum(jnp.sum(values * values, axis=1, keepdims=True), axis=0, keepdims=True)
            found = found + jnp.where((lane == place + offset) & (row == 0), square, 0.0)
    squares[...] = found


def directions_step(payload, grads, firsts, seconds, masters):
    vmem = pl.BlockSpec(memory_space=pltpu.VMEM)
    return pl.pallas_call(
        directions_body,
        out_shape=jax.ShapeDtypeStruct((8, 128), F32),
        in_specs=[vmem] * 17,
        out_specs=vmem,
        compiler_params=pltpu.CompilerParams(vmem_limit_bytes=16 * 2**20),
        cost_estimate=cost("directions"),
        name="directions",
    )(payload, *grads, *firsts, *seconds, *masters)


def moments_step(payload, grads, firsts, seconds, masters, marker):
    vmem = pl.BlockSpec(memory_space=pltpu.VMEM)
    shapes = [jax.ShapeDtypeStruct(master.shape, F32) for master in masters]
    outs = pl.pallas_call(
        moments_body,
        out_shape=tuple(shapes * 3),
        in_specs=[vmem] * 21,
        out_specs=(vmem,) * 15,
        compiler_params=pltpu.CompilerParams(vmem_limit_bytes=16 * 2**20),
        cost_estimate=cost("moments"),
        name="moments",
    )(payload, *grads, *firsts, *seconds, *masters, marker)
    return outs[0:5], outs[5:10], outs[10:15]


def weights_body(*refs):
    squares, refs = refs[0], refs[1:]
    directions, masters, outs, lows = refs[0:4], refs[4:8], refs[8:12], refs[12:16]
    norms = refs[16]
    norms[...] = jnp.zeros_like(norms)
    weight = jnp.sqrt(squares[0:1, 4:8])
    update = jnp.sqrt(squares[0:1, 0:4])
    for place in range(4):
        ratio = MATRIX_RATE * (weight[:, place : place + 1] / update[:, place : place + 1])
        new = masters[place][...] - ratio * directions[place][...]
        outs[place][...] = new
        lows[place][...] = new.astype(BF16)
    norms[0:1, 0:4] = weight
    norms[1:2, 0:4] = update


def weights_step(squares, directions, masters):
    vmem = pl.BlockSpec(memory_space=pltpu.VMEM)
    outs = pl.pallas_call(
        weights_body,
        out_shape=tuple(jax.ShapeDtypeStruct(m.shape, F32) for m in masters)
        + tuple(jax.ShapeDtypeStruct(m.shape, BF16) for m in masters)
        + (jax.ShapeDtypeStruct((8, 128), F32),),
        in_specs=[vmem] * 9,
        out_specs=(vmem,) * 9,
        compiler_params=pltpu.CompilerParams(vmem_limit_bytes=60 * 2**20),
        cost_estimate=cost("weights"),
        name="weights",
    )(squares, *directions, *masters)
    return outs[0:4], outs[4:8], outs[8]


BOTH = ("batch", "head")
PARTNER = 1
ACROSS = 2


def dot(a, b, dims):
    return lax.dot_general(a, b, (dims, ((), ())), preferred_element_type=F32)


def swap(values, axis, mask):
    size = lax.axis_size(axis)
    return lax.ppermute(values, axis, [(place, place ^ mask) for place in range(size)])


def partner(values):
    return swap(values, "head", PARTNER)


def across(values):
    return swap(values, "head", ACROSS)


def batch_masks():
    return [1 << bit for bit in range((lax.axis_size("batch") - 1).bit_length())][::-1]


class Chain:
    def __init__(self, scalars, chunk, order, chips):
        self.scalars, self.values, self.order, self.chips = scalars, chunk[None], list(order), chips
        self.masks, self.flip, self.arrived = [0], 0, None

    def start(self):
        axis, mask = self.order.pop(0)
        self.flip = mask if not self.chips else (2 * mask if axis == "batch" else 1)
        self.arrived = swap(self.values, axis, mask)

    def pair(self):
        return self.values, self.arrived

    def take(self, joined):
        self.values = joined
        self.masks = self.masks + [mask ^ self.flip for mask in self.masks]
        self.arrived = None
        if self.order:
            self.start()

    def drain(self, left):
        while len(self.order) > left:
            self.take(join(self.scalars, [self.pair()], [0])[0])

    def halves(self, joined, orders):
        chains = []
        for values, order in zip(joined, orders):
            chain = Chain(self.scalars, values[0], order, self.chips)
            chain.values = values
            chain.masks = self.masks + [mask ^ self.flip for mask in self.masks]
            chain.start()
            chains.append(chain)
        return chains

    def parts(self, multiple, kinds=1):
        rows = self.values.shape[1] // kinds
        source = CHIP if self.chips else ROW
        arrays, masks = [self.values], [self.masks]
        if self.arrived is not None:
            arrays.append(self.arrived)
            masks.append([mask ^ self.flip for mask in self.masks])
        if rows % multiple == 0:
            return source, arrays, masks
        chunks = [array[r] for array in arrays for r in range(array.shape[0])]
        order = [mask for group in masks for mask in group]
        count = len(order)
        natural = jnp.stack([chunks[order.index(place)] for place in range(count)])
        size = 1
        while size < count:
            cut = natural.reshape((-1, 2, size) + natural.shape[1:])
            flipped = jnp.concatenate([cut[:, 1:], cut[:, :1]], axis=1)
            cut = jnp.where((self.scalars[source] & size) != 0, flipped, cut)
            natural = cut.reshape(natural.shape)
            size *= 2
        natural = natural.reshape(count, kinds, rows, -1).transpose(1, 0, 2, 3)
        return None, [natural.reshape(1, kinds * count * rows, -1)], [[0]]


def join_all(scalars, chains, extra=(), markers=()):
    pairs = [chain.pair() for chain in chains] + list(extra)
    joined = join(scalars, pairs, [0] * len(pairs), markers)
    for chain, values in zip(chains, joined):
        chain.take(values)
    return joined[len(chains) :]


def bit_source(bit):
    axis, mask = bit
    return (ROW, mask.bit_length() - 1) if axis == "batch" else (SIDE, 0)


class Reduce:
    def __init__(self, bits, order, *values):
        self.left, self.order, self.values, self.full = list(bits), list(order), values, None

    def split(self):
        bit = self.order.pop(0)
        size = 1 << (len(self.left) - 1 - self.left.index(bit))
        self.left.remove(bit)
        self.bit = bit
        return (*bit_source(bit), size)

    def begin(self, scalars):
        self.full = self.split()
        self.sources = []
        for values in self.values:
            self.send(scalars, values)

    def send(self, scalars, values):
        which, shift, size = self.full
        bit = (scalars[which] >> shift) & 1
        rows = values.shape[1:]
        cut = values.reshape((-1, 2, size) + rows)
        sent = lax.dynamic_index_in_dim(cut, 1 - bit, 1, keepdims=False).reshape((-1,) + rows)
        self.sources.append((values, swap(sent.astype(BF16), *self.bit)))

    def begin_with(self, *pairs):
        self.full = None
        self.sources = [(kept, swap(sent, *self.bit)) for sent, kept in pairs]

    def add_source(self, sent, kept):
        self.sources.append((kept, swap(sent, *self.bit)))

    @property
    def kept(self):
        return self.sources[0][0]


def reduce_all(scalars, chains, markers=()):
    plans, inputs, outs = [], [scalars], []
    for chain in chains:
        full = chain.full
        for source in chain.sources:
            inputs += source
        plan = chain.split() if chain.order else None
        plans.append(([full] * len(chain.sources), plan))
        count, rows, _ = chain.sources[0][1].shape
        columns = sum(arrived.shape[2] for _, arrived in chain.sources)
        if plan is None:
            outs.append(shape((count, rows, columns), F32))
        else:
            outs.append(shape((count // 2, rows, columns), BF16))
            outs.append(shape((count // 2, rows, columns), F32))
    found = list(call(partial(reduce_body, plans), inputs, outs, [], 16, "add_arrived", markers=markers))
    for chain, (_, plan) in zip(chains, plans):
        if plan is None:
            chain.values = found.pop(0)
        else:
            sent, kept = found.pop(0), found.pop(0)
            chain.begin_with((sent, kept))


def all_sum(values):
    for mask in (PARTNER, ACROSS):
        values = values + swap(values, "head", mask)
    masks = batch_masks()[::-1]
    if len(masks) % 2:
        values = values + swap(values, "batch", masks[0])
        masks = masks[1:]
    for low, high in zip(masks[::2], masks[1::2]):
        near = values + swap(values, "batch", low)
        far = swap(values, "batch", high) + swap(values, "batch", low | high)
        values = near + far
    return values


def block_permutation(slot, to_owner):
    rows, heads = lax.axis_size("batch"), lax.axis_size("head")
    total = rows * heads
    pairs = []
    for owner in range(total):
        place = (3 * owner + slot) % total
        holder = (place % rows) * heads + place // rows
        pairs.append((holder, owner) if to_owner else (owner, holder))
    return pairs


def holder_place():
    return lax.axis_size("batch") * lax.axis_index("head") + lax.axis_index("batch")


def blocks_to_holders(shard):
    blocks = shard.reshape(3, -1, D)
    return [lax.ppermute(blocks[slot], BOTH, block_permutation(slot, False)) for slot in range(3)]


def blocks_to_owners(blocks):
    total = lax.axis_size("batch") * lax.axis_size("head")
    place = holder_place()
    arrived = []
    for slot in range(3):
        kind = ((slot + 3 * total - place) * total) % 3
        sent = lax.dynamic_index_in_dim(blocks, kind, 0, keepdims=False)
        arrived.append(lax.ppermute(sent, BOTH, block_permutation(slot, True)))
    return jnp.concatenate(arrived, axis=0)


def on_device(
    tokens,
    cotangent,
    lengths,
    input_weight,
    output_weight,
    expand_weight,
    contract_weight,
    vector_params,
    input_first,
    input_second,
    output_first,
    output_second,
    expand_first,
    expand_second,
    contract_first,
    contract_second,
    vector_first,
    vector_second,
):
    rows_of_devices = lax.axis_size("batch")
    head_count = lax.axis_size("head")
    chips = rows_of_devices * head_count // 2
    here = lax.axis_index("head")
    core = here % 2
    side = here // 2
    width = D // head_count
    heads = width // HD
    piece = tokens.shape[0]
    docs = lengths.shape[1]
    hidden_block = FF // (2 * chips)
    half = FF // 2
    out_rows = output_weight.shape[0]
    total_devices = rows_of_devices * head_count
    batch_bits = [("batch", mask) for mask in batch_masks()]
    far, near = batch_bits[:-1], batch_bits[-1]
    side_bit = ("head", ACROSS)
    bits = batch_bits + [side_bit]
    bias_contract = vector_params[7 * D : 8 * D]

    def by_core(mine, other, axis):
        high = core == 1
        return jnp.stack([jnp.where(high, other, mine), jnp.where(high, mine, other)], axis=axis)

    def pick(values, index, axis):
        return lax.dynamic_index_in_dim(values, index, axis, keepdims=False)

    scalars, sequences = Places(), Places(lengths)
    lines = vector_params.reshape(VECTOR_ROWS, 128)

    *in_blocks, expand_low, output_mine, output_cut, contract_low, normed_own = prepare(
        scalars, input_weight, expand_weight, output_weight, contract_weight, tokens, lines
    )
    in_arrived = [
        lax.ppermute(block, BOTH, block_permutation(slot, False)) for slot, block in enumerate(in_blocks)
    ]
    expands = Chain(scalars, expand_low, far, True)
    expands.start()
    normed_across = across(normed_own)
    contract_cut = contract_low.reshape(out_rows, chips, 2, hidden_block)
    sent = jnp.concatenate([pick(contract_cut, 1 - core, 2).reshape(out_rows, half), output_cut], axis=1)
    columns_arrived = partner(sent)
    contract_mine = pick(contract_cut, core, 2).reshape(out_rows, half)
    contract_shard = by_core(contract_mine, columns_arrived[:, :half], 0).reshape(2 * out_rows, half)
    output_shard = by_core(output_mine, columns_arrived[:, half:], 0).reshape(2 * out_rows, 2 * width)
    contracts = Chain(scalars, contract_shard, [near, side_bit] + far, True)
    contracts.start()

    def cores_first(vectors):
        hidden = vectors[:, 8 * D :].reshape(-1, chips, 2, hidden_block).transpose(0, 2, 1, 3)
        return jnp.concatenate([vectors[:, : 8 * D], hidden.reshape(-1, FF)], axis=1).reshape(-1, VECTOR_ROWS, 128)

    def cores_back(rows):
        vectors = rows.reshape(-1, 8 * D + FF)
        hidden = vectors[:, 8 * D :].reshape(-1, 2, chips, hidden_block).transpose(0, 2, 1, 3)
        return jnp.concatenate([vectors[:, : 8 * D], hidden.reshape(-1, FF)], axis=1)

    vector_state = cores_first(jnp.stack([vector_first, vector_second, vector_params]))
    kinds = block_kinds(scalars, in_arrived, total_devices).reshape(-1, D)
    inputs = Chain(scalars, kinds, batch_bits, False)
    outputs = Chain(scalars, output_shard, far + [side_bit, near], True)
    inputs.start()
    outputs.start()
    inputs.drain(2)
    outputs.drain(3)
    join_all(scalars, [inputs, outputs, contracts], (), (expands.arrived,))
    expands.drain(1)
    (normed_mine,) = join_all(
        scalars, [inputs, outputs, contracts, expands], [(normed_own, normed_across)], (vector_state,)
    )
    contracts.drain(1)
    normed_other = partner(normed_mine)

    projected, weight_in, joined = project(
        scalars,
        normed_mine,
        normed_other,
        lines,
        *inputs.parts(8, 3),
        [outputs.pair(), expands.pair()],
        [0, 2],
        (),
    )
    outputs.take(joined[0])
    expands = expands.halves(joined[1:], ([near, side_bit], [side_bit, near]))

    blocks = 4 * piece // BLOCK
    before = attention_forward(sequences, projected, heads, docs, piece, (0, blocks // 2))
    join_all(scalars, [*expands, contracts, outputs], (), (before[0],))
    _, logs, keep_t, send_t = attention_forward(
        sequences, projected, heads, docs, piece, (blocks // 2, blocks), before, (contracts.values,)
    )
    across_t = across(send_t)
    cotangent_other = partner(cotangent)
    *branch_sent, branch_kept, output_own, output_across = branch(
        scalars,
        keep_t,
        across_t,
        *outputs.parts(16),
        [expands[0].arrived, expands[1].arrived],
    )
    resid_mid, *normed_two = middle_norm(
        scalars,
        tokens,
        branch_kept,
        [partner(rows) for rows in branch_sent],
        lines,
        (contracts.arrived,),
    )
    arrived_two = [partner(rows) for rows in normed_two]

    found = [chain.parts(16) for chain in expands]
    activated, slopes, expand_half, normed_pair, cotangent_pair = rise(
        scalars,
        (*normed_two, *arrived_two),
        (cotangent, cotangent_other),
        vector_state[2],
        [part[0] for part in found],
        [part[1] for part in found],
        [part[2] for part in found],
    )
    grad_hidden, normed_sent, normed_kept, out_sent, out_kept, hidden_sums = feed_forward(
        scalars, activated, slopes, expand_half, cotangent_pair, *contracts.parts(16)
    )
    normed_arrived = partner(normed_sent)
    out_arrived = partner(out_sent)
    block_out = (resid_mid + out_kept + out_arrived.astype(F32) + bias_contract).astype(BF16)

    expand_sum = Reduce(bits, [near] + far[-1:] + [side_bit] + far[:-1][::-1])
    contract_sum = Reduce(bits, far[-1:] + [side_bit, near] + far[:-1][::-1])
    output_sum = Reduce(bits, [side_bit] + far[-1:])
    sums = [expand_sum, contract_sum]
    aligned = hidden_block % 8 == 0 and 2 * out_rows % 8 == 0
    if aligned:
        plans = [chain.split() for chain in sums]
        contract_sum.begin_with(
            product_grad(scalars, cotangent_pair, activated, plans[1], chips, "contract_gradient")
        )
    else:
        expand_total = dot(grad_hidden, normed_pair, ((0,), (0,))).astype(BF16)
        contract_total = dot(cotangent_pair, activated, ((0,), (0,))).astype(BF16)
        expand_sum.values = (expand_total.reshape(chips, hidden_block, D),)
        contract_sum.values = (contract_total.reshape(chips, 2 * out_rows, half),)
        for chain in sums:
            chain.begin(scalars)
    grad_mid, grad_branch, middle_sums = norm_backward(
        middle_body,
        [normed_kept, normed_arrived, resid_mid, cotangent],
        lines,
        (F32, BF16),
        "middle_gradient",
        (contract_sum.kept,),
    )
    grads = (grad_branch, partner(grad_branch))
    if aligned:
        expand_sum.begin_with(
            product_grad(scalars, grad_hidden, normed_pair, plans[0], chips, "expand_gradient")
        )

    grad_keep_t, grad_sent_t = head_grads(scalars, grads, output_own, output_across, (expand_sum.kept,))
    grad_arrived_t = across(grad_sent_t)
    output_found = output_weight_grad(
        scalars, grads, keep_t, across_t, output_sum.split() if aligned else None, chips, (grad_sent_t,)
    )
    if aligned:
        output_sum.begin_with(output_found)
    else:
        output_sum.values = (output_found[0].reshape(chips, 2 * out_rows, 2 * width),)
        output_sum.begin(scalars)
    inputs = (sequences, projected, (keep_t, send_t), (grad_keep_t, grad_arrived_t), logs, heads, docs, piece)
    *before, _ = attention_backward(
        *inputs, (0, blocks // 2), (), [block_out, *(chain.kept for chain in (*sums, output_sum))]
    )
    reduce_all(scalars, [*sums, output_sum], (before[0],))
    grad_heads, _, _, head_sums = attention_backward(
        *inputs, (blocks // 2, blocks), before, [chain.kept for chain in sums]
    )

    contract_sum.sources += output_sum.sources
    reduce_all(scalars, sums, (grad_heads,))
    *far_sent, far_kept = first_grads(
        scalars, grad_heads, weight_in, (3, 2), (), [chain.kept for chain in sums]
    )
    far_arrived = [partner(rows) for rows in far_sent]
    in_found = input_weight_grad(
        scalars, grad_heads, normed_mine, normed_other, rows_of_devices, D // total_devices
    )
    in_sum = Reduce(batch_bits, far[-1:] + [near] + far[:-1][::-1])
    if len(in_found) == 2:
        in_sum.split()
        in_sum.begin_with(in_found)
    else:
        in_sum.values = (in_found[0].reshape(3 * rows_of_devices, -1, D),)
        in_sum.begin(scalars)
    reduce_all(scalars, sums, (in_sum.kept,))
    reduce_all(scalars, [in_sum], (sums[0].kept,))
    reduced_far, near_sent, near_kept = first_grads(
        scalars, grad_heads, weight_in, (1, 0), (far_kept, *far_arrived), (in_sum.kept,)
    )
    first_arrived = across(reduced_far)
    near_arrived = partner(near_sent)
    while sums[0].order:
        reduce_all(scalars, sums, (reduced_far,))
    reduce_all(scalars, sums, (reduced_far,))
    while in_sum.order:
        reduce_all(scalars, [in_sum], (expand_sum.values,))
    reduce_all(scalars, [in_sum], (first_arrived,))
    input_piece_grad = blocks_to_owners(in_sum.values)
    expand_grad = expand_sum.values.reshape(hidden_block, D)
    contract_mixed = contract_sum.values[0, :, :half]
    output_mixed = contract_sum.values[0, :, half:]

    def columns_other(mixed, parts):
        cut = mixed.reshape(2, out_rows, parts, -1)
        return pick(cut, core, 0), partner(pick(cut, 1 - core, 0))

    contract_grad = by_core(*columns_other(contract_mixed, chips), 2).reshape(out_rows, -1)
    output_grad = by_core(*columns_other(output_mixed, 2), 2).reshape(out_rows, -1)
    input_grad, first_sums = norm_backward(
        first_body,
        [near_kept, near_arrived, first_arrived, tokens, grad_mid],
        lines,
        (BF16,),
        "first_gradient",
    )

    masters = (input_weight, output_weight, expand_weight, contract_weight)
    gradients = [part.values for part in (in_sum, expand_sum, contract_sum)]
    payload = all_sum(
        make_payload(scalars, gradients, first_sums, middle_sums, head_sums, hidden_sums)
    )
    vector_grads = payload[:VECTOR_ROWS]
    grad_norm = jnp.sqrt(payload[VECTOR_ROWS, 0] + jnp.sum(vector_grads * vector_grads))
    shard_grads = (input_piece_grad, output_grad, expand_grad, contract_grad)
    firsts = (input_first, output_first, expand_first, contract_first)
    seconds = (input_second, output_second, expand_second, contract_second)
    squares = directions_step(payload, shard_grads, firsts, seconds, masters)
    first_new, second_new, directions = moments_step(
        payload,
        shard_grads,
        (*firsts, vector_state[0]),
        (*seconds, vector_state[1]),
        (*masters, vector_state[2]),
        squares,
    )
    squares = all_sum(squares)
    vector_news = cores_back(jnp.stack([first_new[4], second_new[4], directions[4]]))
    news, lows, norms = weights_step(squares, directions[:4], masters)
    results = []
    for position in range(4):
        results += [first_new[position], second_new[position], news[position], lows[position]]
    return (
        block_out,
        input_grad,
        grad_norm,
        norms[:2, :4].reshape(8),
        *results,
        vector_news[0],
        vector_news[1],
        vector_news[2],
    )


def solution(mesh):
    split = P(BOTH, None)
    return jax.shard_map(
        on_device,
        mesh=mesh,
        in_specs=(split, split, P("batch", None)) + (split,) * 4 + (P(),) + (split,) * 8 + (P(), P()),
        out_specs=(split, split, P(), P()) + (split,) * 16 + (P(), P(), P()),
        check_vma=False,
    )
```

profile of v0, /device:TPU:0, one launch (start us, length us, event | category | flops | bytes accessed | tf_op | source)
XLA Modules:
  0.0 289.2 jit_solution(10585844648629526287)
XLA Ops:
  0.7 3.0 %prepare.1 = (bf16[24,768]{1,0:T(8,128)(2,1)}, bf16[24,768]{1,0:T(8,128)(2,1)}, bf16[24,768]{1,0:T(8,128)(2,1)}, bf16[96,768]{1,0:T(8,128)(2,1)}, bf16[24,384]{1...) custom-call(f32[72,768]{1,0:T(8,128)} %refs_5_.5, ...), custom_call_target="tpu_custom_call" | custom-call | flops 2800000000 | tf_op jit(solution)/shard_map/prepare/pallas_call | solution.py:332
  8.9 5.7 %collective-permute-start.1 = (bf16[24,768]{1,0:T(8,128)(2,1)}, bf16[24,768]{1,0:T(8,128)(2,1)S(1)}, u32[]{:S(2)}, u32[]{:S(2)}) collective-permute-start(bf16[24,768]{1,0:T(8,128)(2,1)} %get-tuple-element.143), channel_id=1, source_target_pairs={{0,4},{1,16},{2,28},{3,9},{4,21},{5,2},{6,14},{7,26},{8,7},{9,19},... | collective-permute-start | bytes 110600 | tf_op jit(solution)/shard_map/ppermute | solution.py:1401
  14.6 4.0 %collective-permute-start.2 = (bf16[24,768]{1,0:T(8,128)(2,1)}, bf16[24,768]{1,0:T(8,128)(2,1)S(1)}, u32[]{:S(2)}, u32[]{:S(2)}) collective-permute-start(bf16[24,768]{1,0:T(8,128)(2,1)} %get-tuple-element.144), channel_id=1, source_target_pairs={{0,8},{1,20},{2,1},{3,13},{4,25},{5,6},{6,18},{7,30},{8,11},{9,23}... | collective-permute-start | bytes 110600 | tf_op jit(solution)/shard_map/ppermute | solution.py:1401
  21.7 4.0 %collective-permute-start.3 = (bf16[1,72,768]{2,1,0:T(8,128)(2,1)S(1)}, bf16[1,72,768]{2,1,0:T(8,128)(2,1)S(1)}, u32[]{:S(2)}, u32[]{:S(2)}) collective-permute-start(bf16[1,72,768]{2,1,0:T(8,128)(2,1)S(1)} %bitcast.88), channel_id=1, source_target_pairs={{0,16},{4,20},{8,24},{12,28},{16,0},{20,4},{24,8},{28,12},{1,17},{... | collective-permute-start | bytes 331784 | tf_op jit(solution)/shard_map/ppermute | solution.py:1155
  26.6 6.7 %collective-permute-done.5.refs_3_ = bf16[1,48,384]{2,1,0:T(8,128)(2,1)S(1)} collective-permute-done((bf16[1,48,384]{2,1,0:T(8,128)(2,1)S(1)}, bf16[1,48,384]{2,1,0:T(8,128)(2,1)S(1)}, u32[]{:S(2)}, u32[]{:S(2)}) %collective-permute-start.5) | collective-permute-done | bytes 36896 | tf_op jit(solution)/shard_map/ppermute | solution.py:1155
  33.4 3.0 %collective-permute-start.10 = (bf16[2,48,1536]{2,1,0:T(8,128)(2,1)S(1)}, bf16[2,48,1536]{2,1,0:T(8,128)(2,1)S(1)}, u32[]{:S(2)}, u32[]{:S(2)}) collective-permute-start(bf16[2,48,1536]{2,1,0:T(8,128)(2,1)S(1)} %get-tuple-element.151.refs_4_), channel_id=1, source_target_pairs={{0,2},{1,3},{2,0},{3,1},{4,6},{5,7},{6,4},{7,5},{8,10},{9,11},{10,... | collective-permute-start | bytes 884744 | tf_op jit(solution)/shard_map/ppermute | solution.py:1155
  38.9 6.0 %collective-permute-done.9.refs_3_ = bf16[2,48,384]{2,1,0:T(8,128)(2,1)S(1)} collective-permute-done((bf16[2,48,384]{2,1,0:T(8,128)(2,1)S(1)}, bf16[2,48,384]{2,1,0:T(8,128)(2,1)S(1)}, u32[]{:S(2)}, u32[]{:S(2)}) %collective-permute-start.9) | collective-permute-done | bytes 73760 | tf_op jit(solution)/shard_map/ppermute | solution.py:1155
  51.0 4.2 %collective-permute-done.14.refs_6_ = bf16[4,48,384]{2,1,0:T(8,128)(2,1)S(1)} collective-permute-done((bf16[4,48,384]{2,1,0:T(8,128)(2,1)S(1)}, bf16[4,48,384]{2,1,0:T(8,128)(2,1)S(1)}, u32[]{:S(2)}, u32[]{:S(2)}) %collective-permute-start.14) | collective-permute-done | bytes 147488 | tf_op jit(solution)/shard_map/ppermute | solution.py:1155
  55.2 6.2 %collective-permute-done.15.refs_8_ = bf16[2,96,768]{2,1,0:T(8,128)(2,1)S(1)} collective-permute-done((bf16[2,96,768]{2,1,0:T(8,128)(2,1)S(1)}, bf16[2,96,768]{2,1,0:T(8,128)(2,1)S(1)}, u32[]{:S(2)}, u32[]{:S(2)}) %collective-permute-start.15) | collective-permute-done | bytes 294944 | tf_op jit(solution)/shard_map/ppermute | solution.py:1155
  61.4 3.0 %project.1 = (bf16[2048,768]{1,0:T(8,128)(2,1)S(1)}, bf16[768,768]{1,0:T(8,128)(2,1)S(1)}, bf16[8,48,384]{2,1,0:T(8,128)(2,1)S(1)}, bf16[4,48,768]{2,1,0:T(8,128)(2,1)S(1)}, bf16[4,48,768]{2,1,0:T(8,128)(2,1)S(1)}) custom-call(bf16[1024,768]{1,0:T(8,128)(2,1)S(1)} %get-tuple-element.153.refs_0_.refs_1_, ...), custom_call_target="tpu_custom_call" | custom-call | flops 5000000000 | tf_op jit(solution)/shard_map/project/pallas_call | solution.py:332
  67.0 7.2 %attention_forward.2 = (bf16[192,2048]{1,0:T(8,128)(2,1)S(1)}, f32[8,2048]{1,0:T(8,128)S(1)}) custom-call(s32[1,3]{1,0:T(1,128)S(1)} %copy-done.16, bf16[2048,768]{1,0:T(8,128)(2,1)S(1)} %get-tuple-element.157.refs_1_), custom_call_target="tpu_custom_call" | custom-call | flops 8000000000 | tf_op jit(solution)/shard_map/attention_forward/pallas_call | solution.py:332
  74.2 4.1 %collective-permute-done.18.refs_5_ = bf16[4,48,1536]{2,1,0:T(8,128)(2,1)S(1)} collective-permute-done((bf16[4,48,1536]{2,1,0:T(8,128)(2,1)S(1)}, bf16[4,48,1536]{2,1,0:T(8,128)(2,1)S(1)}, u32[]{:S(2)}, u32[]{:S(2)}) %collective-permute-start.18) | collective-permute-done | bytes 589856 | tf_op jit(solution)/shard_map/ppermute | solution.py:1155
  80.6 7.4 %attention_forward.3 = (bf16[192,2048]{1,0:T(8,128)(2,1)S(1)}, f32[8,2048]{1,0:T(8,128)S(1)}, bf16[192,1024]{1,0:T(8,128)(2,1)S(1)}, bf16[192,1024]{1,0:T(8,128)(2,1)S(1)}) custom-call(s32[1,3]{1,0:T(1,128)S(1)} %copy-done.16, bf16[2048,768]{1,0:T(8,128)(2,1)S(1)} %get-tuple-element.157.refs_1_, ...), custom_call_target="tpu_custom_call", output_to_operand_aliasing={{0}: (2, {}), {1}: (3, {})} | custom-call | flops 8000000000 | tf_op jit(solution)/shard_map/attention_forward/pallas_call | solution.py:332
  89.9 11.5 %collective-permute-done.20.refs_1_.refs_3_ = bf16[192,1024]{1,0:T(8,128)(2,1)S(1)} collective-permute-done((bf16[192,1024]{1,0:T(8,128)(2,1)S(1)}, bf16[192,1024]{1,0:T(8,128)(2,1)S(1)}, u32[]{:S(2)}, u32[]{:S(2)}) %collective-permute-start.20) | collective-permute-done | bytes 393248 | tf_op jit(solution)/shard_map/ppermute | solution.py:1155
  110.0 6.3 %rise.1 = (bf16[1024,1536]{1,0:T(8,128)(2,1)S(1)}, f32[1024,1536]{1,0:T(8,128)S(1)}, bf16[1536,768]{1,0:T(8,128)(2,1)S(1)}, bf16[1024,768]{1,0:T(8,128)(2,1)S(1)}, bf16[1024,768]{1,0:T(8,128)(2,1)S(1)}) custom-call(bf16[256,768]{1,0:T(8,128)(2,1)S(1)} %get-tuple-element.174.refs_0_, bf16[256,768]{1,0:T(8,128)(2,1)S(1)} %get-tuple-element.175.refs_1_, ...), custom_call_target="tpu_custom_call" | custom-call | flops 100000000 | tf_op jit(solution)/shard_map/rise/pallas_call | solution.py:332
  116.2 8.9 %feed_forward.1 = (bf16[1024,1536]{1,0:T(8,128)(2,1)S(1)}, bf16[512,768]{1,0:T(8,128)(2,1)S(1)}, f32[512,768]{1,0:T(8,128)S(1)}, bf16[512,768]{1,0:T(8,128)(2,1)...) custom-call(bf16[1024,1536]{1,0:T(8,128)(2,1)S(1)} %get-tuple-element.176.refs_0_.refs_1_, ...), custom_call_target="tpu_custom_call" | custom-call | flops 11000000512 | tf_op jit(solution)/shard_map/feed_forward/pallas_call | solution.py:332
  125.4 3.0 %contract_gradient.1 = (bf16[8,48,1536]{2,1,0:T(8,128)(2,1)S(1)}, f32[8,48,1536]{2,1,0:T(8,128)S(1)}) custom-call(bf16[1024,768]{1,0:T(8,128)(2,1)S(1)} %get-tuple-element.179.refs_3_.refs_0_, bf16[1024,1536]{1,0:T(8,128)(2,1)S(1)} %get-tuple-element.176.refs_0_.refs_1_), custom_call_target="tpu_custom_call" | custom-call | flops 400000000 | tf_op jit(solution)/shard_map/contract_gradient/pallas_call | solution.py:332
  131.6 3.0 %expand_gradient.1 = (bf16[8,96,768]{2,1,0:T(8,128)(2,1)S(1)}, f32[8,96,768]{2,1,0:T(8,128)S(1)}) custom-call(bf16[1024,1536]{1,0:T(8,128)(2,1)S(1)} %get-tuple-element.188.refs_0_, bf16[1024,768]{1,0:T(8,128)(2,1)S(1)} %get-tuple-element.189.refs_1_), custom_call_target="tpu_custom_call" | custom-call | flops 400000000 | tf_op jit(solution)/shard_map/expand_gradient/pallas_call | solution.py:332
  141.3 8.4 %collective-permute-done.32.refs_5_ = bf16[192,1024]{1,0:T(8,128)(2,1)S(1)} collective-permute-done((bf16[192,1024]{1,0:T(8,128)(2,1)S(1)}, bf16[192,1024]{1,0:T(8,128)(2,1)S(1)}, u32[]{:S(2)}, u32[]{:S(2)}) %collective-permute-start.32) | collective-permute-done | bytes 393248 | tf_op jit(solution)/shard_map/ppermute | solution.py:1155
  149.7 14.1 %attention_backward.2 = (bf16[2048,768]{1,0:T(8,128)(2,1)S(1)}, f32[2048,256]{1,0:T(8,128)S(1)}, f32[2048,256]{1,0:T(8,128)S(1)}, f32[8,256]{1,0:T(8,128)}) custom-call(s32[1,3]{1,0:T(1,128)S(1)} %copy-done.16, bf16[2048,768]{1,0:T(8,128)(2,1)S(1)} %get-tuple-element.157.refs_1_, bf16[192,1024]{1,0:T(8,128)(2,1)S(1)} %get-tuple-element.165.refs_0_.refs_2_, ...), custom_call_target="tpu_custom_call" | custom-call | flops 2000000000 | tf_op jit(solution)/shard_map/attention_backward/pallas_call | solution.py:332
  167.7 14.5 %attention_backward.3 = (bf16[2048,768]{1,0:T(8,128)(2,1)S(1)}, f32[2048,256]{1,0:T(8,128)S(1)}, f32[2048,256]{1,0:T(8,128)S(1)}, f32[8,256]{1,0:T(8,128)S(1)}) custom-call(s32[1,3]{1,0:T(1,128)S(1)} %copy-done.16, bf16[2048,768]{1,0:T(8,128)(2,1)S(1)} %get-tuple-element.157.refs_1_, ...), custom_call_target="tpu_custom_call", output_to_operand_aliasing={{0}: (7, {}), {1}: (8, {}), {2}: (9, {})} | custom-call | flops 2000000000 | tf_op jit(solution)/shard_map/attention_backward/pallas_call | solution.py:332
  183.7 3.7 %input_weight_gradient.1 = (bf16[12,24,768]{2,1,0:T(8,128)(2,1)}, f32[12,24,768]{2,1,0:T(8,128)S(1)}) custom-call(bf16[2048,768]{1,0:T(8,128)(2,1)S(1)} %get-tuple-element.203.refs_6_.refs_0_, bf16[1024,768]{1,0:T(8,128)(2,1)S(1)} %get-tuple-element.153.refs_0_.refs_1_, bf16[1024,768]{1,0:T(8,128)(2,1)S(1)} %collective-permute-done.12.refs_1_.refs_2_), custom_call_target="tpu_custom_call" | custom-call | flops 1000000000 | tf_op jit(solution)/shard_map/input_weight_gradient/pallas_call | solution.py:332
  191.6 3.0 %collective-permute-done.42.refs_1_ = bf16[2,96,768]{2,1,0:T(8,128)(2,1)S(1)} collective-permute-done((bf16[2,96,768]{2,1,0:T(8,128)(2,1)S(1)}, bf16[2,96,768]{2,1,0:T(8,128)(2,1)S(1)}, u32[]{:S(2)}, u32[]{:S(2)}) %collective-permute-start.42) | collective-permute-done | bytes 294944 | tf_op jit(solution)/shard_map/ppermute | solution.py:1155
  196.2 7.4 %collective-permute-start.48 = (bf16[1,48,1920]{2,1,0:T(8,128)(2,1)}, bf16[1,48,1920]{2,1,0:T(8,128)(2,1)}, u32[]{:S(2)}, u32[]{:S(2)}) collective-permute-start(bf16[1,48,1920]{2,1,0:T(8,128)(2,1)} %get-tuple-element.228), channel_id=1, source_target_pairs={{0,16},{4,20},{8,24},{12,28},{16,0},{20,4},{24,8},{28,12},{1,17},{... | collective-permute-start | bytes 552968 | tf_op jit(solution)/shard_map/ppermute | solution.py:1155
  209.4 3.7 %first_norm_gradient.3 = (bf16[512,768]{1,0:T(8,128)(2,1)}, bf16[512,768]{1,0:T(8,128)(2,1)}, f32[512,768]{1,0:T(8,128)S(1)}) custom-call(bf16[2048,768]{1,0:T(8,128)(2,1)S(1)} %get-tuple-element.203.refs_6_.refs_0_, bf16[768,768]{1,0:T(8,128)(2,1)S(1)} %copy-done.1, f32[512,768]{1,0:T(8,128)S(1)} %copy-done.9, ...), custom_call_target="tpu_custom_call" | custom-call | flops 500000000 | tf_op jit(solution)/shard_map/first_norm_gradient/pallas_call | solution.py:332
  222.3 6.4 %collective-permute-done.49.refs_1_ = bf16[3,24,768]{2,1,0:T(8,128)(2,1)S(1)} collective-permute-done((bf16[3,24,768]{2,1,0:T(8,128)(2,1)S(1)}, bf16[3,24,768]{2,1,0:T(8,128)(2,1)S(1)}, u32[]{:S(2)}, u32[]{:S(2)}) %collective-permute-start.49) | collective-permute-done | bytes 110624 | tf_op jit(solution)/shard_map/ppermute | solution.py:1155
  235.8 3.1 %collective-permute-start.50 = (f32[80,128]{1,0:T(8,128)S(1)}, f32[80,128]{1,0:T(8,128)}, u32[]{:S(2)}, u32[]{:S(2)}) collective-permute-start(f32[80,128]{1,0:T(8,128)S(1)} %payload.1), channel_id=1, source_target_pairs={{0,1},{1,0},{2,3},{3,2},{4,5},{5,4},{6,7},{7,6},{8,9},{9,8},{10,11... | collective-permute-start | bytes 122888 | tf_op jit(solution)/shard_map/ppermute | solution.py:1155
  241.9 4.2 %collective-permute-start.58 = (f32[24,768]{1,0:T(8,128)}, f32[24,768]{1,0:T(8,128)S(1)}, u32[]{:S(2)}, u32[]{:S(2)}) collective-permute-start(f32[24,768]{1,0:T(8,128)} %get-tuple-element.265), channel_id=1, source_target_pairs={{8,0},{20,1},{1,2},{13,3},{25,4},{6,5},{18,6},{30,7},{11,8},{23,9}... | collective-permute-start | bytes 221192 | tf_op jit(solution)/shard_map/ppermute | solution.py:1343
  251.6 3.4 %collective-permute-done.52 = f32[80,128]{1,0:T(8,128)S(1)} collective-permute-done((f32[80,128]{1,0:T(8,128)S(1)}, f32[80,128]{1,0:T(8,128)S(1)}, u32[]{:S(2)}, u32[]{:S(2)}) %collective-permute-start.52) | collective-permute-done | bytes 40992 | tf_op jit(solution)/shard_map/ppermute | solution.py:1155
  255.2 3.6 %collective-permute-start.54 = (f32[80,128]{1,0:T(8,128)S(1)}, f32[80,128]{1,0:T(8,128)S(1)}, u32[]{:S(2)}, u32[]{:S(2)}) collective-permute-start(f32[80,128]{1,0:T(8,128)S(1)} %add.102), channel_id=1, source_target_pairs={{0,16},{4,20},{8,24},{12,28},{16,0},{20,4},{24,8},{28,12},{1,17},{... | collective-permute-start | bytes 122888 | tf_op jit(solution)/shard_map/ppermute | solution.py:1155
  261.5 3.1 %collective-permute-done.55 = f32[80,128]{1,0:T(8,128)S(1)} collective-permute-done((f32[80,128]{1,0:T(8,128)S(1)}, f32[80,128]{1,0:T(8,128)S(1)}, u32[]{:S(2)}, u32[]{:S(2)}) %collective-permute-start.55) | collective-permute-done | bytes 40992 | tf_op jit(solution)/shard_map/ppermute | solution.py:1155
  277.7 3.1 %collective-permute-start.66 = (f32[8,128]{1,0:T(8,128)S(1)}, f32[8,128]{1,0:T(8,128)S(1)}, u32[]{:S(2)}, u32[]{:S(2)}) collective-permute-start(f32[8,128]{1,0:T(8,128)S(1)} %add.116), channel_id=1, source_target_pairs={{0,24},{4,28},{8,16},{12,20},{16,8},{20,12},{24,0},{28,4},{1,25},{... | collective-permute-start | bytes 12296 | tf_op jit(solution)/shard_map/ppermute | solution.py:1155
  (289 shorter events, 106.2 us)
Async XLA Ops:
  7.0 18.7 %collective-permute-start.4 = (bf16[24,1920]{1,0:T(8,128)(2,1)S(1)}, bf16[24,1920]{1,0:T(8,128)(2,1)S(1)}, u32[]{:S(2)}, u32[]{:S(2)}) collective-permute-start(bf16[24,1920]{1,0:T(8,128)(2,1)S(1)} %pad_maximum_fusion.6), channel_id=1, source_target_pairs={{0,1},{1,0},{2,3},{3,2},{4,5},{5,4},{6,7},{7,6},{8,9},{9,8},{10,11... | collective-permute-start | bytes 276488 | tf_op jit(solution)/shard_map/ppermute | solution.py:1155
  7.5 12.9 %collective-permute-start = (bf16[24,768]{1,0:T(8,128)(2,1)}, bf16[24,768]{1,0:T(8,128)(2,1)S(1)}, u32[]{:S(2)}, u32[]{:S(2)}) collective-permute-start(bf16[24,768]{1,0:T(8,128)(2,1)} %get-tuple-element.142), channel_id=1, source_target_pairs={{0,0},{1,12},{2,24},{3,5},{4,17},{5,29},{6,10},{7,22},{8,3},{9,15}... | collective-permute-start | bytes 110600 | tf_op jit(solution)/shard_map/ppermute | solution.py:1401
  18.6 14.8 %collective-permute-start.7 = (bf16[1,96,768]{2,1,0:T(8,128)(2,1)}, bf16[1,96,768]{2,1,0:T(8,128)(2,1)S(1)}, u32[]{:S(2)}, u32[]{:S(2)}) collective-permute-start(bf16[1,96,768]{2,1,0:T(8,128)(2,1)} %bitcast.86), channel_id=1, source_target_pairs={{0,16},{4,20},{8,24},{12,28},{16,0},{20,4},{24,8},{28,12},{1,17},{... | collective-permute-start | bytes 442376 | tf_op jit(solution)/shard_map/ppermute | solution.py:1155
  20.4 25.2 %collective-permute-start.11 = (bf16[512,768]{1,0:T(8,128)(2,1)}, bf16[512,768]{1,0:T(8,128)(2,1)S(1)}, u32[]{:S(2)}, u32[]{:S(2)}) collective-permute-start(bf16[512,768]{1,0:T(8,128)(2,1)} %get-tuple-element.152.refs_8_), channel_id=1, source_target_pairs={{0,2},{1,3},{2,0},{3,1},{4,6},{5,7},{6,4},{7,5},{8,10},{9,11},{10,... | collective-permute-start | bytes 2359304 | tf_op jit(solution)/shard_map/ppermute | solution.py:1155
  33.4 12.1 %collective-permute-start.10 = (bf16[2,48,1536]{2,1,0:T(8,128)(2,1)S(1)}, bf16[2,48,1536]{2,1,0:T(8,128)(2,1)S(1)}, u32[]{:S(2)}, u32[]{:S(2)}) collective-permute-start(bf16[2,48,1536]{2,1,0:T(8,128)(2,1)S(1)} %get-tuple-element.151.refs_4_), channel_id=1, source_target_pairs={{0,2},{1,3},{2,0},{3,1},{4,6},{5,7},{6,4},{7,5},{8,10},{9,11},{10,... | collective-permute-start | bytes 884744 | tf_op jit(solution)/shard_map/ppermute | solution.py:1155
  45.7 15.6 %collective-permute-start.12 = (bf16[1024,768]{1,0:T(8,128)(2,1)S(1)}, bf16[1024,768]{1,0:T(8,128)(2,1)S(1)}, u32[]{:S(2)}, u32[]{:S(2)}) collective-permute-start(bf16[1024,768]{1,0:T(8,128)(2,1)S(1)} %get-tuple-element.153.refs_0_.refs_1_), channel_id=1, source_target_pairs={{0,1},{1,0},{2,3},{3,2},{4,5},{5,4},{6,7},{7,6},{8,9},{9,8},{10,11... | collective-permute-start | bytes 4718600 | tf_op jit(solution)/shard_map/ppermute | solution.py:1155
  45.8 15.6 %collective-permute-start.13 = (bf16[4,72,768]{2,1,0:T(8,128)(2,1)S(1)}, bf16[4,72,768]{2,1,0:T(8,128)(2,1)S(1)}, u32[]{:S(2)}, u32[]{:S(2)}) collective-permute-start(bf16[4,72,768]{2,1,0:T(8,128)(2,1)S(1)} %get-tuple-element.154.refs_3_), channel_id=1, source_target_pairs={{0,4},{4,0},{8,12},{12,8},{16,20},{20,16},{24,28},{28,24},{1,5},{5... | collective-permute-start | bytes 1327112 | tf_op jit(solution)/shard_map/ppermute | solution.py:1155
  48.2 13.2 %collective-permute-start.15 = (bf16[2,96,768]{2,1,0:T(8,128)(2,1)S(1)}, bf16[2,96,768]{2,1,0:T(8,128)(2,1)S(1)}, u32[]{:S(2)}, u32[]{:S(2)}) collective-permute-start(bf16[2,96,768]{2,1,0:T(8,128)(2,1)S(1)} %get-tuple-element.156.refs_7_), channel_id=1, source_target_pairs={{0,8},{4,12},{8,0},{12,4},{16,24},{20,28},{24,16},{28,20},{1,9},{5... | collective-permute-start | bytes 884744 | tf_op jit(solution)/shard_map/ppermute | solution.py:1155
  49.9 28.4 %collective-permute-start.18 = (bf16[4,48,1536]{2,1,0:T(8,128)(2,1)S(1)}, bf16[4,48,1536]{2,1,0:T(8,128)(2,1)S(1)}, u32[]{:S(2)}, u32[]{:S(2)}) collective-permute-start(bf16[4,48,1536]{2,1,0:T(8,128)(2,1)S(1)} %get-tuple-element.162.refs_4_), channel_id=1, source_target_pairs={{0,16},{4,20},{8,24},{12,28},{16,0},{20,4},{24,8},{28,12},{1,17},{... | collective-permute-start | bytes 1769480 | tf_op jit(solution)/shard_map/ppermute | solution.py:1155
  64.4 13.9 %collective-permute-start.16 = (bf16[4,48,768]{2,1,0:T(8,128)(2,1)S(1)}, bf16[4,48,768]{2,1,0:T(8,128)(2,1)S(1)}, u32[]{:S(2)}, u32[]{:S(2)}) collective-permute-start(bf16[4,48,768]{2,1,0:T(8,128)(2,1)S(1)} %get-tuple-element.160.refs_0_), channel_id=1, source_target_pairs={{0,4},{4,0},{8,12},{12,8},{16,20},{20,16},{24,28},{28,24},{1,5},{5... | collective-permute-start | bytes 884744 | tf_op jit(solution)/shard_map/ppermute | solution.py:1155
  64.9 13.4 %collective-permute-start.17 = (bf16[4,48,768]{2,1,0:T(8,128)(2,1)S(1)}, bf16[4,48,768]{2,1,0:T(8,128)(2,1)S(1)}, u32[]{:S(2)}, u32[]{:S(2)}) collective-permute-start(bf16[4,48,768]{2,1,0:T(8,128)(2,1)S(1)} %get-tuple-element.161.refs_2_), channel_id=1, source_target_pairs={{0,2},{1,3},{2,0},{3,1},{4,6},{5,7},{6,4},{7,5},{8,10},{9,11},{10,... | collective-permute-start | bytes 884744 | tf_op jit(solution)/shard_map/ppermute | solution.py:1155
  65.7 13.3 %collective-permute-start.19 = (bf16[8,48,384]{2,1,0:T(8,128)(2,1)S(1)}, bf16[8,48,384]{2,1,0:T(8,128)(2,1)S(1)}, u32[]{:S(2)}, u32[]{:S(2)}) collective-permute-start(bf16[8,48,384]{2,1,0:T(8,128)(2,1)S(1)} %get-tuple-element.163.refs_6_), channel_id=1, source_target_pairs={{0,4},{4,0},{8,12},{12,8},{16,20},{20,16},{24,28},{28,24},{1,5},{5... | collective-permute-start | bytes 884744 | tf_op jit(solution)/shard_map/ppermute | solution.py:1155
  79.2 22.1 %collective-permute-start.21 = (bf16[8,48,768]{2,1,0:T(8,128)(2,1)S(1)}, bf16[8,48,768]{2,1,0:T(8,128)(2,1)S(1)}, u32[]{:S(2)}, u32[]{:S(2)}) collective-permute-start(bf16[8,48,768]{2,1,0:T(8,128)(2,1)S(1)} %get-tuple-element.168.refs_7_), channel_id=1, source_target_pairs={{0,2},{1,3},{2,0},{3,1},{4,6},{5,7},{6,4},{7,5},{8,10},{9,11},{10,... | collective-permute-start | bytes 1769480 | tf_op jit(solution)/shard_map/ppermute | solution.py:1155
  80.3 21.0 %collective-permute-start.22 = (bf16[8,48,768]{2,1,0:T(8,128)(2,1)S(1)}, bf16[8,48,768]{2,1,0:T(8,128)(2,1)S(1)}, u32[]{:S(2)}, u32[]{:S(2)}) collective-permute-start(bf16[8,48,768]{2,1,0:T(8,128)(2,1)S(1)} %get-tuple-element.169.refs_9_), channel_id=1, source_target_pairs={{0,4},{4,0},{8,12},{12,8},{16,20},{20,16},{24,28},{28,24},{1,5},{5... | collective-permute-start | bytes 1769480 | tf_op jit(solution)/shard_map/ppermute | solution.py:1155
  80.6 26.3 %collective-permute-start.25 = (bf16[8,48,1536]{2,1,0:T(8,128)(2,1)S(1)}, bf16[8,48,1536]{2,1,0:T(8,128)(2,1)S(1)}, u32[]{:S(2)}, u32[]{:S(2)}) collective-permute-start(bf16[8,48,1536]{2,1,0:T(8,128)(2,1)S(1)} %get-tuple-element.164.refs_4_), channel_id=1, source_target_pairs={{0,8},{4,12},{8,0},{12,4},{16,24},{20,28},{24,16},{28,20},{1,9},{5... | collective-permute-start | bytes 3538952 | tf_op jit(solution)/shard_map/ppermute | solution.py:1155
  88.0 13.3 %collective-permute-start.20 = (bf16[192,1024]{1,0:T(8,128)(2,1)S(1)}, bf16[192,1024]{1,0:T(8,128)(2,1)S(1)}, u32[]{:S(2)}, u32[]{:S(2)}) collective-permute-start(bf16[192,1024]{1,0:T(8,128)(2,1)S(1)} %get-tuple-element.166.refs_3_), channel_id=1, source_target_pairs={{0,2},{1,3},{2,0},{3,1},{4,6},{5,7},{6,4},{7,5},{8,10},{9,11},{10,... | collective-permute-start | bytes 1179656 | tf_op jit(solution)/shard_map/ppermute | solution.py:1155
  134.6 29.2 %collective-permute-start.33 = (bf16[8,96,768]{2,1,0:T(8,128)(2,1)S(1)}, bf16[8,96,768]{2,1,0:T(8,128)(2,1)S(1)}, u32[]{:S(2)}, u32[]{:S(2)}) collective-permute-start(bf16[8,96,768]{2,1,0:T(8,128)(2,1)S(1)} %get-tuple-element.198), channel_id=1, source_target_pairs={{0,4},{4,0},{8,12},{12,8},{16,20},{20,16},{24,28},{28,24},{1,5},{5... | collective-permute-start | bytes 3538952 | tf_op jit(solution)/shard_map/ppermute | solution.py:1155
  136.2 27.9 %collective-permute-start.34 = (bf16[8,48,1536]{2,1,0:T(8,128)(2,1)S(1)}, bf16[8,48,1536]{2,1,0:T(8,128)(2,1)S(1)}, u32[]{:S(2)}, u32[]{:S(2)}) collective-permute-start(bf16[8,48,1536]{2,1,0:T(8,128)(2,1)S(1)} %get-tuple-element.199), channel_id=1, source_target_pairs={{0,8},{4,12},{8,0},{12,4},{16,24},{20,28},{24,16},{28,20},{1,9},{5... | collective-permute-start | bytes 3538952 | tf_op jit(solution)/shard_map/ppermute | solution.py:1155
  139.6 24.6 %collective-permute-start.35 = (bf16[8,48,384]{2,1,0:T(8,128)(2,1)S(1)}, bf16[8,48,384]{2,1,0:T(8,128)(2,1)S(1)}, u32[]{:S(2)}, u32[]{:S(2)}) collective-permute-start(bf16[8,48,384]{2,1,0:T(8,128)(2,1)S(1)} %get-tuple-element.200), channel_id=1, source_target_pairs={{0,2},{1,3},{2,0},{3,1},{4,6},{5,7},{6,4},{7,5},{8,10},{9,11},{10,... | collective-permute-start | bytes 884744 | tf_op jit(solution)/shard_map/ppermute | solution.py:1155
  164.9 17.7 %collective-permute-start.36 = (bf16[4,96,768]{2,1,0:T(8,128)(2,1)S(1)}, bf16[4,96,768]{2,1,0:T(8,128)(2,1)S(1)}, u32[]{:S(2)}, u32[]{:S(2)}) collective-permute-start(bf16[4,96,768]{2,1,0:T(8,128)(2,1)S(1)} %get-tuple-element.205), channel_id=1, source_target_pairs={{0,8},{4,12},{8,0},{12,4},{16,24},{20,28},{24,16},{28,20},{1,9},{5... | collective-permute-start | bytes 1769480 | tf_op jit(solution)/shard_map/ppermute | solution.py:1155
  166.4 16.2 %collective-permute-start.37 = (bf16[4,48,1536]{2,1,0:T(8,128)(2,1)S(1)}, bf16[4,48,1536]{2,1,0:T(8,128)(2,1)S(1)}, u32[]{:S(2)}, u32[]{:S(2)}) collective-permute-start(bf16[4,48,1536]{2,1,0:T(8,128)(2,1)S(1)} %get-tuple-element.206), channel_id=1, source_target_pairs={{0,2},{1,3},{2,0},{3,1},{4,6},{5,7},{6,4},{7,5},{8,10},{9,11},{10,... | collective-permute-start | bytes 1769480 | tf_op jit(solution)/shard_map/ppermute | solution.py:1155
  167.1 15.6 %collective-permute-start.38 = (bf16[4,48,384]{2,1,0:T(8,128)(2,1)S(1)}, bf16[4,48,384]{2,1,0:T(8,128)(2,1)S(1)}, u32[]{:S(2)}, u32[]{:S(2)}) collective-permute-start(bf16[4,48,384]{2,1,0:T(8,128)(2,1)S(1)} %get-tuple-element.208), channel_id=1, source_target_pairs={{0,8},{4,12},{8,0},{12,4},{16,24},{20,28},{24,16},{28,20},{1,9},{5... | collective-permute-start | bytes 442376 | tf_op jit(solution)/shard_map/ppermute | solution.py:1155
  187.3 16.2 %collective-permute-start.41 = (bf16[12,24,768]{2,1,0:T(8,128)(2,1)}, bf16[12,24,768]{2,1,0:T(8,128)(2,1)}, u32[]{:S(2)}, u32[]{:S(2)}) collective-permute-start(bf16[12,24,768]{2,1,0:T(8,128)(2,1)} %get-tuple-element.215), channel_id=1, source_target_pairs={{0,8},{4,12},{8,0},{12,4},{16,24},{20,28},{24,16},{28,20},{1,9},{5... | collective-permute-start | bytes 1327112 | tf_op jit(solution)/shard_map/ppermute | solution.py:1155
  191.0 17.0 %collective-permute-start.39 = (bf16[256,768]{1,0:T(8,128)(2,1)}, bf16[256,768]{1,0:T(8,128)(2,1)}, u32[]{:S(2)}, u32[]{:S(2)}) collective-permute-start(bf16[256,768]{1,0:T(8,128)(2,1)} %get-tuple-element.212), channel_id=1, source_target_pairs={{0,1},{1,0},{2,3},{3,2},{4,5},{5,4},{6,7},{7,6},{8,9},{9,8},{10,11... | collective-permute-start | bytes 1179656 | tf_op jit(solution)/shard_map/ppermute | solution.py:1155
  191.1 17.0 %collective-permute-start.40 = (bf16[256,768]{1,0:T(8,128)(2,1)}, bf16[256,768]{1,0:T(8,128)(2,1)}, u32[]{:S(2)}, u32[]{:S(2)}) collective-permute-start(bf16[256,768]{1,0:T(8,128)(2,1)} %get-tuple-element.213), channel_id=1, source_target_pairs={{0,1},{1,0},{2,3},{3,2},{4,5},{5,4},{6,7},{7,6},{8,9},{9,8},{10,11... | collective-permute-start | bytes 1179656 | tf_op jit(solution)/shard_map/ppermute | solution.py:1155
  196.2 19.8 %collective-permute-start.48 = (bf16[1,48,1920]{2,1,0:T(8,128)(2,1)}, bf16[1,48,1920]{2,1,0:T(8,128)(2,1)}, u32[]{:S(2)}, u32[]{:S(2)}) collective-permute-start(bf16[1,48,1920]{2,1,0:T(8,128)(2,1)} %get-tuple-element.228), channel_id=1, source_target_pairs={{0,16},{4,20},{8,24},{12,28},{16,0},{20,4},{24,8},{28,12},{1,17},{... | collective-permute-start | bytes 552968 | tf_op jit(solution)/shard_map/ppermute | solution.py:1155
  203.5 12.4 %collective-permute-start.47 = (bf16[1,96,768]{2,1,0:T(8,128)(2,1)}, bf16[1,96,768]{2,1,0:T(8,128)(2,1)}, u32[]{:S(2)}, u32[]{:S(2)}) collective-permute-start(bf16[1,96,768]{2,1,0:T(8,128)(2,1)} %get-tuple-element.226), channel_id=1, source_target_pairs={{0,16},{4,20},{8,24},{12,28},{16,0},{20,4},{24,8},{28,12},{1,17},{... | collective-permute-start | bytes 442376 | tf_op jit(solution)/shard_map/ppermute | solution.py:1155
  206.7 12.4 %collective-permute-start.46 = (bf16[6,24,768]{2,1,0:T(8,128)(2,1)}, bf16[6,24,768]{2,1,0:T(8,128)(2,1)}, u32[]{:S(2)}, u32[]{:S(2)}) collective-permute-start(bf16[6,24,768]{2,1,0:T(8,128)(2,1)} %get-tuple-element.225), channel_id=1, source_target_pairs={{0,4},{4,0},{8,12},{12,8},{16,20},{20,16},{24,28},{28,24},{1,5},{5... | collective-permute-start | bytes 663560 | tf_op jit(solution)/shard_map/ppermute | solution.py:1155
  213.1 16.2 %collective-permute-start.45 = (bf16[512,768]{1,0:T(8,128)(2,1)}, bf16[512,768]{1,0:T(8,128)(2,1)S(1)}, u32[]{:S(2)}, u32[]{:S(2)}) collective-permute-start(bf16[512,768]{1,0:T(8,128)(2,1)} %get-tuple-element.222.refs_4_), channel_id=1, source_target_pairs={{0,2},{1,3},{2,0},{3,1},{4,6},{5,7},{6,4},{7,5},{8,10},{9,11},{10,... | collective-permute-start | bytes 2359304 | tf_op jit(solution)/shard_map/ppermute | solution.py:1155
  213.9 17.6 %collective-permute-start.44 = (bf16[512,768]{1,0:T(8,128)(2,1)}, bf16[512,768]{1,0:T(8,128)(2,1)S(1)}, u32[]{:S(2)}, u32[]{:S(2)}) collective-permute-start(bf16[512,768]{1,0:T(8,128)(2,1)} %get-tuple-element.221), channel_id=1, source_target_pairs={{0,1},{1,0},{2,3},{3,2},{4,5},{5,4},{6,7},{7,6},{8,9},{9,8},{10,11... | collective-permute-start | bytes 2359304 | tf_op jit(solution)/shard_map/ppermute | solution.py:1155
  230.0 19.0 %collective-permute-start.56 = (f32[24,768]{1,0:T(8,128)}, f32[24,768]{1,0:T(8,128)S(1)}, u32[]{:S(2)}, u32[]{:S(2)}) collective-permute-start(f32[24,768]{1,0:T(8,128)} %get-tuple-element.267), channel_id=1, source_target_pairs={{0,0},{12,1},{24,2},{5,3},{17,4},{29,5},{10,6},{22,7},{3,8},{15,9}... | collective-permute-start | bytes 221192 | tf_op jit(solution)/shard_map/ppermute | solution.py:1343
  241.9 17.5 %collective-permute-start.58 = (f32[24,768]{1,0:T(8,128)}, f32[24,768]{1,0:T(8,128)S(1)}, u32[]{:S(2)}, u32[]{:S(2)}) collective-permute-start(f32[24,768]{1,0:T(8,128)} %get-tuple-element.265), channel_id=1, source_target_pairs={{8,0},{20,1},{1,2},{13,3},{25,4},{6,5},{18,6},{30,7},{11,8},{23,9}... | collective-permute-start | bytes 221192 | tf_op jit(solution)/shard_map/ppermute | solution.py:1343
  (83 other events, 941.6 us)
where the time goes:
time: 295 us; the launch traced here: 289 us
  Pallas kernels  101 us (34%)
  starting transfers between devices  81.3 us (28%)
  waiting for transfers between devices  80.8 us (27%)
  local copies, waits for them, and re-layouts  14.8 us (5%)
  other arithmetic  7.09 us (2%)
  between operations  4.34 us (1%)
    pallas_call x29, Pallas kernels, call(): pl.pallas_call(whole, out_shape=tuple(outputs), in_specs=[SMEM] * len(lea...  90.7 us
    ppermute x61, waiting for transfers between devices, swap(): lax.ppermute(values, axis, [(place, place ^ mask) for place in range(size)])  79.8 us
    ppermute x61, starting transfers between devices, swap(): lax.ppermute(values, axis, [(place, place ^ mask) for place in range(size)])  64.3 us
    ppermute x3, starting transfers between devices, on_device(): lax.ppermute(block, BOTH, block_permutation(slot, False))  11.1 us
    unnamed x99, local copies, waits for them, and re-layouts  7.05 us
    ppermute x3, starting transfers between devices, blocks_to_owners(): arrived.append(lax.ppermute(sent, BOTH, block_permutation(slot, True)))  5.94 us
  transfers between devices with their start and end apart: 67, of which 28 were waited for; matrix products, arithmetic and copies ran while one was open for 3% of the time, Pallas kernels for 26%

commit v1 on v0

--- a/solution.py
+++ b/solution.py
@@ -893,7 +893,7 @@
     out[VECTOR_ROWS : VECTOR_ROWS + 1, :] = jnp.where(lane == 0, total, 0.0)
 
 
-def make_payload(scalars, gradients, first, middle, heads, hidden):
+def make_payload(scalars, gradients, first, middle, heads, hidden, markers):
     return call(
         partial(payload_body, hidden.shape[1] // 128),
         [scalars, *gradients, first, middle, heads, hidden],
@@ -901,6 +901,7 @@
         [],
         12,
         "payload",
+        markers,
     )[0]
 
 
@@ -1006,7 +1007,7 @@
 
 def norm_backward(body, arrays, lines, outputs, name, markers=()):
     rows = arrays[0].shape[0]
-    step = min(128, rows)
+    step = min(256, rows)
     tile = pl.BlockSpec((step, D), lambda i: (i, 0))
     row = pl.BlockSpec(lines.shape, lambda i: (0, 0))
     sums = pl.BlockSpec((24, 128), lambda i: (0, 0))
@@ -1022,7 +1023,7 @@
         + (jax.ShapeDtypeStruct((24, 128), F32),),
         in_specs=[tile] * len(arrays) + [row] + [LEFT] * len(markers),
         out_specs=tuple(tile for _ in outputs) + (sums,),
-        compiler_params=pltpu.CompilerParams(vmem_limit_bytes=10 * 2**20),
+        compiler_params=pltpu.CompilerParams(vmem_limit_bytes=14 * 2**20),
         cost_estimate=cost(name),
         name=name,
     )(*arrays, lines, *markers)
@@ -1593,7 +1594,15 @@
     masters = (input_weight, output_weight, expand_weight, contract_weight)
     gradients = [part.values for part in (in_sum, expand_sum, contract_sum)]
     payload = all_sum(
-        make_payload(scalars, gradients, first_sums, middle_sums, head_sums, hidden_sums)
+        make_payload(
+            scalars,
+            gradients,
+            first_sums,
+            middle_sums,
+            head_sums,
+            hidden_sums,
+            (input_piece_grad, contract_grad, output_grad),
+        )
     )
     vector_grads = payload[:VECTOR_ROWS]
     grad_norm = jnp.sqrt(payload[VECTOR_ROWS, 0] + jnp.sum(vector_grads * vector_grads))

time: 295 us -> 292 us (0.990)
  starting transfers between devices: 81.3 us -> 76 us
  Pallas kernels: 101 us -> 105 us
  waiting for transfers between devices: 80.8 us -> 83.8 us
    ppermute x61, starting transfers between devices: 64.3 us -> 56.4 us  [swap(): lax.ppermute(values, axis, [(place, place ^ mask) for place in range(size)])]
    pallas_call x29, Pallas kernels: 90.7 us -> 93.6 us  [call(): pl.pallas_call(whole, out_shape=tuple(outputs), in_specs=[SMEM] * len(lea...]
    ppermute x61, waiting for transfers between devices: 79.8 us -> 82.7 us  [swap(): lax.ppermute(values, axis, [(place, place ^ mask) for place in range(size)])]
  transfers between devices with their start and end apart: 67 -> 67, of which waited for: 28 -> 29; matrix products, arithmetic and copies ran while one was open for 3% -> 2% of each run, Pallas kernels for 26% -> 28%
where the time goes in v1:
time: 292 us; the launch traced here: 287 us
  Pallas kernels  105 us (36%)
  waiting for transfers between devices  83.8 us (29%)
  starting transfers between devices  76 us (26%)
  local copies, waits for them, and re-layouts  13.4 us (5%)
  other arithmetic  4.64 us (2%)
  between operations  4.47 us (2%)
    pallas_call x29, Pallas kernels, call(): pl.pallas_call(whole, out_shape=tuple(outputs), in_specs=[SMEM] * len(lea...  93.6 us
    ppermute x61, waiting for transfers between devices, swap(): lax.ppermute(values, axis, [(place, place ^ mask) for place in range(size)])  82.7 us
    ppermute x61, starting transfers between devices, swap(): lax.ppermute(values, axis, [(place, place ^ mask) for place in range(size)])  56.4 us
    ppermute x3, starting transfers between devices, on_device(): lax.ppermute(block, BOTH, block_permutation(slot, False))  11.1 us
    ppermute x3, starting transfers between devices, blocks_to_owners(): arrived.append(lax.ppermute(sent, BOTH, block_permutation(slot, True)))  8.54 us
    unnamed x99, local copies, waits for them, and re-layouts  7.28 us
  transfers between devices with their start and end apart: 67, of which 29 were waited for; matrix products, arithmetic and copies ran while one was open for 2% of the time, Pallas kernels for 28%

profile of v1, /device:TPU:0, one launch (start us, length us, event | category | flops | bytes accessed | tf_op | source)
XLA Modules:
  0.0 286.8 jit_solution(9159465864481942570)
XLA Ops:
  0.7 3.0 %prepare.1 = (bf16[24,768]{1,0:T(8,128)(2,1)}, bf16[24,768]{1,0:T(8,128)(2,1)}, bf16[24,768]{1,0:T(8,128)(2,1)}, bf16[96,768]{1,0:T(8,128)(2,1)}, bf16[24,384]{1...) custom-call(f32[72,768]{1,0:T(8,128)} %refs_5_.5, ...), custom_call_target="tpu_custom_call" | custom-call | flops 2800000000 | tf_op jit(solution)/shard_map/prepare/pallas_call | solution.py:332
  8.9 5.7 %collective-permute-start.1 = (bf16[24,768]{1,0:T(8,128)(2,1)}, bf16[24,768]{1,0:T(8,128)(2,1)S(1)}, u32[]{:S(2)}, u32[]{:S(2)}) collective-permute-start(bf16[24,768]{1,0:T(8,128)(2,1)} %get-tuple-element.143), channel_id=1, source_target_pairs={{0,4},{1,16},{2,28},{3,9},{4,21},{5,2},{6,14},{7,26},{8,7},{9,19},... | collective-permute-start | bytes 110600 | tf_op jit(solution)/shard_map/ppermute | solution.py:1402
  14.6 4.0 %collective-permute-start.2 = (bf16[24,768]{1,0:T(8,128)(2,1)}, bf16[24,768]{1,0:T(8,128)(2,1)S(1)}, u32[]{:S(2)}, u32[]{:S(2)}) collective-permute-start(bf16[24,768]{1,0:T(8,128)(2,1)} %get-tuple-element.144), channel_id=1, source_target_pairs={{0,8},{1,20},{2,1},{3,13},{4,25},{5,6},{6,18},{7,30},{8,11},{9,23}... | collective-permute-start | bytes 110600 | tf_op jit(solution)/shard_map/ppermute | solution.py:1402
  21.7 4.0 %collective-permute-start.3 = (bf16[1,72,768]{2,1,0:T(8,128)(2,1)S(1)}, bf16[1,72,768]{2,1,0:T(8,128)(2,1)S(1)}, u32[]{:S(2)}, u32[]{:S(2)}) collective-permute-start(bf16[1,72,768]{2,1,0:T(8,128)(2,1)S(1)} %bitcast.88), channel_id=1, source_target_pairs={{0,16},{4,20},{8,24},{12,28},{16,0},{20,4},{24,8},{28,12},{1,17},{... | collective-permute-start | bytes 331784 | tf_op jit(solution)/shard_map/ppermute | solution.py:1156
  26.6 6.7 %collective-permute-done.5.refs_3_ = bf16[1,48,384]{2,1,0:T(8,128)(2,1)S(1)} collective-permute-done((bf16[1,48,384]{2,1,0:T(8,128)(2,1)S(1)}, bf16[1,48,384]{2,1,0:T(8,128)(2,1)S(1)}, u32[]{:S(2)}, u32[]{:S(2)}) %collective-permute-start.5) | collective-permute-done | bytes 36896 | tf_op jit(solution)/shard_map/ppermute | solution.py:1156
  33.4 3.0 %collective-permute-start.10 = (bf16[2,48,1536]{2,1,0:T(8,128)(2,1)S(1)}, bf16[2,48,1536]{2,1,0:T(8,128)(2,1)S(1)}, u32[]{:S(2)}, u32[]{:S(2)}) collective-permute-start(bf16[2,48,1536]{2,1,0:T(8,128)(2,1)S(1)} %get-tuple-element.151.refs_4_), channel_id=1, source_target_pairs={{0,2},{1,3},{2,0},{3,1},{4,6},{5,7},{6,4},{7,5},{8,10},{9,11},{10,... | collective-permute-start | bytes 884744 | tf_op jit(solution)/shard_map/ppermute | solution.py:1156
  38.9 6.0 %collective-permute-done.9.refs_3_ = bf16[2,48,384]{2,1,0:T(8,128)(2,1)S(1)} collective-permute-done((bf16[2,48,384]{2,1,0:T(8,128)(2,1)S(1)}, bf16[2,48,384]{2,1,0:T(8,128)(2,1)S(1)}, u32[]{:S(2)}, u32[]{:S(2)}) %collective-permute-start.9) | collective-permute-done | bytes 73760 | tf_op jit(solution)/shard_map/ppermute | solution.py:1156
  51.0 4.2 %collective-permute-done.14.refs_6_ = bf16[4,48,384]{2,1,0:T(8,128)(2,1)S(1)} collective-permute-done((bf16[4,48,384]{2,1,0:T(8,128)(2,1)S(1)}, bf16[4,48,384]{2,1,0:T(8,128)(2,1)S(1)}, u32[]{:S(2)}, u32[]{:S(2)}) %collective-permute-start.14) | collective-permute-done | bytes 147488 | tf_op jit(solution)/shard_map/ppermute | solution.py:1156
  55.2 6.2 %collective-permute-done.15.refs_8_ = bf16[2,96,768]{2,1,0:T(8,128)(2,1)S(1)} collective-permute-done((bf16[2,96,768]{2,1,0:T(8,128)(2,1)S(1)}, bf16[2,96,768]{2,1,0:T(8,128)(2,1)S(1)}, u32[]{:S(2)}, u32[]{:S(2)}) %collective-permute-start.15) | collective-permute-done | bytes 294944 | tf_op jit(solution)/shard_map/ppermute | solution.py:1156
  61.4 3.0 %project.1 = (bf16[2048,768]{1,0:T(8,128)(2,1)S(1)}, bf16[768,768]{1,0:T(8,128)(2,1)S(1)}, bf16[8,48,384]{2,1,0:T(8,128)(2,1)S(1)}, bf16[4,48,768]{2,1,0:T(8,128)(2,1)S(1)}, bf16[4,48,768]{2,1,0:T(8,128)(2,1)S(1)}) custom-call(bf16[1024,768]{1,0:T(8,128)(2,1)S(1)} %get-tuple-element.153.refs_0_.refs_1_, ...), custom_call_target="tpu_custom_call" | custom-call | flops 5000000000 | tf_op jit(solution)/shard_map/project/pallas_call | solution.py:332
  67.0 6.1 %attention_forward.2 = (bf16[192,2048]{1,0:T(8,128)(2,1)S(1)}, f32[8,2048]{1,0:T(8,128)S(1)}) custom-call(s32[1,3]{1,0:T(1,128)S(1)} %copy-done.16, bf16[2048,768]{1,0:T(8,128)(2,1)S(1)} %get-tuple-element.157.refs_1_), custom_call_target="tpu_custom_call" | custom-call | flops 8000000000 | tf_op jit(solution)/shard_map/attention_forward/pallas_call | solution.py:332
  73.2 5.1 %collective-permute-done.18.refs_5_ = bf16[4,48,1536]{2,1,0:T(8,128)(2,1)S(1)} collective-permute-done((bf16[4,48,1536]{2,1,0:T(8,128)(2,1)S(1)}, bf16[4,48,1536]{2,1,0:T(8,128)(2,1)S(1)}, u32[]{:S(2)}, u32[]{:S(2)}) %collective-permute-start.18) | collective-permute-done | bytes 589856 | tf_op jit(solution)/shard_map/ppermute | solution.py:1156
  80.6 9.8 %attention_forward.3 = (bf16[192,2048]{1,0:T(8,128)(2,1)S(1)}, f32[8,2048]{1,0:T(8,128)S(1)}, bf16[192,1024]{1,0:T(8,128)(2,1)S(1)}, bf16[192,1024]{1,0:T(8,128)(2,1)S(1)}) custom-call(s32[1,3]{1,0:T(1,128)S(1)} %copy-done.16, bf16[2048,768]{1,0:T(8,128)(2,1)S(1)} %get-tuple-element.157.refs_1_, ...), custom_call_target="tpu_custom_call", output_to_operand_aliasing={{0}: (2, {}), {1}: (3, {})} | custom-call | flops 8000000000 | tf_op jit(solution)/shard_map/attention_forward/pallas_call | solution.py:332
  92.3 9.1 %collective-permute-done.20.refs_1_.refs_3_ = bf16[192,1024]{1,0:T(8,128)(2,1)S(1)} collective-permute-done((bf16[192,1024]{1,0:T(8,128)(2,1)S(1)}, bf16[192,1024]{1,0:T(8,128)(2,1)S(1)}, u32[]{:S(2)}, u32[]{:S(2)}) %collective-permute-start.20) | collective-permute-done | bytes 393248 | tf_op jit(solution)/shard_map/ppermute | solution.py:1156
  110.0 6.2 %rise.1 = (bf16[1024,1536]{1,0:T(8,128)(2,1)S(1)}, f32[1024,1536]{1,0:T(8,128)S(1)}, bf16[1536,768]{1,0:T(8,128)(2,1)S(1)}, bf16[1024,768]{1,0:T(8,128)(2,1)S(1)}, bf16[1024,768]{1,0:T(8,128)(2,1)S(1)}) custom-call(bf16[256,768]{1,0:T(8,128)(2,1)S(1)} %get-tuple-element.174.refs_0_, bf16[256,768]{1,0:T(8,128)(2,1)S(1)} %get-tuple-element.175.refs_1_, ...), custom_call_target="tpu_custom_call" | custom-call | flops 100000000 | tf_op jit(solution)/shard_map/rise/pallas_call | solution.py:332
  116.2 8.8 %feed_forward.1 = (bf16[1024,1536]{1,0:T(8,128)(2,1)S(1)}, bf16[512,768]{1,0:T(8,128)(2,1)S(1)}, f32[512,768]{1,0:T(8,128)S(1)}, bf16[512,768]{1,0:T(8,128)(2,1)...) custom-call(bf16[1024,1536]{1,0:T(8,128)(2,1)S(1)} %get-tuple-element.176.refs_0_.refs_1_, ...), custom_call_target="tpu_custom_call" | custom-call | flops 11000000512 | tf_op jit(solution)/shard_map/feed_forward/pallas_call | solution.py:332
  125.3 3.0 %contract_gradient.1 = (bf16[8,48,1536]{2,1,0:T(8,128)(2,1)S(1)}, f32[8,48,1536]{2,1,0:T(8,128)S(1)}) custom-call(bf16[1024,768]{1,0:T(8,128)(2,1)S(1)} %get-tuple-element.179.refs_3_.refs_0_, bf16[1024,1536]{1,0:T(8,128)(2,1)S(1)} %get-tuple-element.176.refs_0_.refs_1_), custom_call_target="tpu_custom_call" | custom-call | flops 400000000 | tf_op jit(solution)/shard_map/contract_gradient/pallas_call | solution.py:332
  131.5 3.0 %expand_gradient.1 = (bf16[8,96,768]{2,1,0:T(8,128)(2,1)S(1)}, f32[8,96,768]{2,1,0:T(8,128)S(1)}) custom-call(bf16[1024,1536]{1,0:T(8,128)(2,1)S(1)} %get-tuple-element.188.refs_0_, bf16[1024,768]{1,0:T(8,128)(2,1)S(1)} %get-tuple-element.189.refs_1_), custom_call_target="tpu_custom_call" | custom-call | flops 400000000 | tf_op jit(solution)/shard_map/expand_gradient/pallas_call | solution.py:332
  141.3 8.3 %collective-permute-done.32.refs_5_ = bf16[192,1024]{1,0:T(8,128)(2,1)S(1)} collective-permute-done((bf16[192,1024]{1,0:T(8,128)(2,1)S(1)}, bf16[192,1024]{1,0:T(8,128)(2,1)S(1)}, u32[]{:S(2)}, u32[]{:S(2)}) %collective-permute-start.32) | collective-permute-done | bytes 393248 | tf_op jit(solution)/shard_map/ppermute | solution.py:1156
  149.6 11.9 %attention_backward.2 = (bf16[2048,768]{1,0:T(8,128)(2,1)S(1)}, f32[2048,256]{1,0:T(8,128)S(1)}, f32[2048,256]{1,0:T(8,128)S(1)}, f32[8,256]{1,0:T(8,128)}) custom-call(s32[1,3]{1,0:T(1,128)S(1)} %copy-done.16, bf16[2048,768]{1,0:T(8,128)(2,1)S(1)} %get-tuple-element.157.refs_1_, bf16[192,1024]{1,0:T(8,128)(2,1)S(1)} %get-tuple-element.165.refs_0_.refs_2_, ...), custom_call_target="tpu_custom_call" | custom-call | flops 2000000000 | tf_op jit(solution)/shard_map/attention_backward/pallas_call | solution.py:332
  167.7 18.6 %attention_backward.3 = (bf16[2048,768]{1,0:T(8,128)(2,1)S(1)}, f32[2048,256]{1,0:T(8,128)S(1)}, f32[2048,256]{1,0:T(8,128)S(1)}, f32[8,256]{1,0:T(8,128)S(1)}) custom-call(s32[1,3]{1,0:T(1,128)S(1)} %copy-done.16, bf16[2048,768]{1,0:T(8,128)(2,1)S(1)} %get-tuple-element.157.refs_1_, ...), custom_call_target="tpu_custom_call", output_to_operand_aliasing={{0}: (7, {}), {1}: (8, {}), {2}: (9, {})} | custom-call | flops 2000000000 | tf_op jit(solution)/shard_map/attention_backward/pallas_call | solution.py:332
  186.9 3.7 %input_weight_gradient.1 = (bf16[12,24,768]{2,1,0:T(8,128)(2,1)}, f32[12,24,768]{2,1,0:T(8,128)S(1)}) custom-call(bf16[2048,768]{1,0:T(8,128)(2,1)S(1)} %get-tuple-element.203.refs_6_.refs_0_, bf16[1024,768]{1,0:T(8,128)(2,1)S(1)} %get-tuple-element.153.refs_0_.refs_1_, bf16[1024,768]{1,0:T(8,128)(2,1)S(1)} %collective-permute-done.12.refs_1_.refs_2_), custom_call_target="tpu_custom_call" | custom-call | flops 1000000000 | tf_op jit(solution)/shard_map/input_weight_gradient/pallas_call | solution.py:332
  194.9 3.7 %collective-permute-done.42.refs_1_ = bf16[2,96,768]{2,1,0:T(8,128)(2,1)S(1)} collective-permute-done((bf16[2,96,768]{2,1,0:T(8,128)(2,1)S(1)}, bf16[2,96,768]{2,1,0:T(8,128)(2,1)S(1)}, u32[]{:S(2)}, u32[]{:S(2)}) %collective-permute-start.42) | collective-permute-done | bytes 294944 | tf_op jit(solution)/shard_map/ppermute | solution.py:1156
  200.3 3.0 %collective-permute-start.48 = (bf16[1,48,1920]{2,1,0:T(8,128)(2,1)}, bf16[1,48,1920]{2,1,0:T(8,128)(2,1)}, u32[]{:S(2)}, u32[]{:S(2)}) collective-permute-start(bf16[1,48,1920]{2,1,0:T(8,128)(2,1)} %get-tuple-element.228), channel_id=1, source_target_pairs={{0,16},{4,20},{8,24},{12,28},{16,0},{20,4},{24,8},{28,12},{1,17},{... | collective-permute-start | bytes 552968 | tf_op jit(solution)/shard_map/ppermute | solution.py:1156
  209.1 3.7 %first_norm_gradient.3 = (bf16[512,768]{1,0:T(8,128)(2,1)}, bf16[512,768]{1,0:T(8,128)(2,1)}, f32[512,768]{1,0:T(8,128)S(1)}) custom-call(bf16[2048,768]{1,0:T(8,128)(2,1)S(1)} %get-tuple-element.203.refs_6_.refs_0_, bf16[768,768]{1,0:T(8,128)(2,1)S(1)} %copy-done.1, f32[512,768]{1,0:T(8,128)S(1)} %copy-done.9, ...), custom_call_target="tpu_custom_call" | custom-call | flops 500000000 | tf_op jit(solution)/shard_map/first_norm_gradient/pallas_call | solution.py:332
  221.7 6.2 %collective-permute-done.49.refs_1_ = bf16[3,24,768]{2,1,0:T(8,128)(2,1)S(1)} collective-permute-done((bf16[3,24,768]{2,1,0:T(8,128)(2,1)S(1)}, bf16[3,24,768]{2,1,0:T(8,128)(2,1)S(1)}, u32[]{:S(2)}, u32[]{:S(2)}) %collective-permute-start.49) | collective-permute-done | bytes 110624 | tf_op jit(solution)/shard_map/ppermute | solution.py:1156
  231.1 6.5 %collective-permute-start.52 = (f32[24,768]{1,0:T(8,128)S(1)}, f32[24,768]{1,0:T(8,128)S(1)}, u32[]{:S(2)}, u32[]{:S(2)}) collective-permute-start(f32[24,768]{1,0:T(8,128)S(1)} %get-tuple-element.265), channel_id=1, source_target_pairs={{8,0},{20,1},{1,2},{13,3},{25,4},{6,5},{18,6},{30,7},{11,8},{23,9}... | collective-permute-start | bytes 221192 | tf_op jit(solution)/shard_map/ppermute | solution.py:1344
  239.0 3.2 %first_gradient.1 = (bf16[512,768]{1,0:T(8,128)(2,1)}, f32[24,128]{1,0:T(8,128)S(1)}) custom-call(f32[512,768]{1,0:T(8,128)S(1)} %copy-done.20, bf16[512,768]{1,0:T(8,128)(2,1)} %collective-permute-done.44.refs_1_, bf16[512,768]{1,0:T(8,128)(2,1)S(1)} %collective-permute-done.45.refs_2_, bf16[512,768]{1,0:T(8,128)(2,1)S(1)} %copy-done.11, ...), custom_call_target="tpu_custom_call" | custom-call | flops 2500000000 | tf_op jit(solution)/shard_map/first_gradient/pallas_call | solution.py:1019
  248.8 3.1 %collective-permute-done.57 = f32[80,128]{1,0:T(8,128)S(1)} collective-permute-done((f32[80,128]{1,0:T(8,128)S(1)}, f32[80,128]{1,0:T(8,128)S(1)}, u32[]{:S(2)}, u32[]{:S(2)}) %collective-permute-start.57) | collective-permute-done | bytes 40992 | tf_op jit(solution)/shard_map/ppermute | solution.py:1156
  252.9 3.4 %collective-permute-start.59 = (f32[80,128]{1,0:T(8,128)S(1)}, f32[80,128]{1,0:T(8,128)S(1)}, u32[]{:S(2)}, u32[]{:S(2)}) collective-permute-start(f32[80,128]{1,0:T(8,128)S(1)} %add.109), channel_id=1, source_target_pairs={{0,16},{4,20},{8,24},{12,28},{16,0},{20,4},{24,8},{28,12},{1,17},{... | collective-permute-start | bytes 122888 | tf_op jit(solution)/shard_map/ppermute | solution.py:1156
  259.1 2.9 %collective-permute-done.60 = f32[80,128]{1,0:T(8,128)S(1)} collective-permute-done((f32[80,128]{1,0:T(8,128)S(1)}, f32[80,128]{1,0:T(8,128)S(1)}, u32[]{:S(2)}, u32[]{:S(2)}) %collective-permute-start.60) | collective-permute-done | bytes 40992 | tf_op jit(solution)/shard_map/ppermute | solution.py:1156
  274.9 3.4 %collective-permute-start.66 = (f32[8,128]{1,0:T(8,128)S(1)}, f32[8,128]{1,0:T(8,128)S(1)}, u32[]{:S(2)}, u32[]{:S(2)}) collective-permute-start(f32[8,128]{1,0:T(8,128)S(1)} %add.116), channel_id=1, source_target_pairs={{0,24},{4,28},{8,16},{12,20},{16,8},{20,12},{24,0},{28,4},{1,25},{... | collective-permute-start | bytes 12296 | tf_op jit(solution)/shard_map/ppermute | solution.py:1156
  (289 shorter events, 103.6 us)
Async XLA Ops:
  7.0 18.7 %collective-permute-start.4 = (bf16[24,1920]{1,0:T(8,128)(2,1)S(1)}, bf16[24,1920]{1,0:T(8,128)(2,1)S(1)}, u32[]{:S(2)}, u32[]{:S(2)}) collective-permute-start(bf16[24,1920]{1,0:T(8,128)(2,1)S(1)} %pad_maximum_fusion.6), channel_id=1, source_target_pairs={{0,1},{1,0},{2,3},{3,2},{4,5},{5,4},{6,7},{7,6},{8,9},{9,8},{10,11... | collective-permute-start | bytes 276488 | tf_op jit(solution)/shard_map/ppermute | solution.py:1156
  7.5 12.9 %collective-permute-start = (bf16[24,768]{1,0:T(8,128)(2,1)}, bf16[24,768]{1,0:T(8,128)(2,1)S(1)}, u32[]{:S(2)}, u32[]{:S(2)}) collective-permute-start(bf16[24,768]{1,0:T(8,128)(2,1)} %get-tuple-element.142), channel_id=1, source_target_pairs={{0,0},{1,12},{2,24},{3,5},{4,17},{5,29},{6,10},{7,22},{8,3},{9,15}... | collective-permute-start | bytes 110600 | tf_op jit(solution)/shard_map/ppermute | solution.py:1402
  18.6 14.8 %collective-permute-start.7 = (bf16[1,96,768]{2,1,0:T(8,128)(2,1)}, bf16[1,96,768]{2,1,0:T(8,128)(2,1)S(1)}, u32[]{:S(2)}, u32[]{:S(2)}) collective-permute-start(bf16[1,96,768]{2,1,0:T(8,128)(2,1)} %bitcast.86), channel_id=1, source_target_pairs={{0,16},{4,20},{8,24},{12,28},{16,0},{20,4},{24,8},{28,12},{1,17},{... | collective-permute-start | bytes 442376 | tf_op jit(solution)/shard_map/ppermute | solution.py:1156
  20.4 25.2 %collective-permute-start.11 = (bf16[512,768]{1,0:T(8,128)(2,1)}, bf16[512,768]{1,0:T(8,128)(2,1)S(1)}, u32[]{:S(2)}, u32[]{:S(2)}) collective-permute-start(bf16[512,768]{1,0:T(8,128)(2,1)} %get-tuple-element.152.refs_8_), channel_id=1, source_target_pairs={{0,2},{1,3},{2,0},{3,1},{4,6},{5,7},{6,4},{7,5},{8,10},{9,11},{10,... | collective-permute-start | bytes 2359304 | tf_op jit(solution)/shard_map/ppermute | solution.py:1156
  33.4 12.1 %collective-permute-start.10 = (bf16[2,48,1536]{2,1,0:T(8,128)(2,1)S(1)}, bf16[2,48,1536]{2,1,0:T(8,128)(2,1)S(1)}, u32[]{:S(2)}, u32[]{:S(2)}) collective-permute-start(bf16[2,48,1536]{2,1,0:T(8,128)(2,1)S(1)} %get-tuple-element.151.refs_4_), channel_id=1, source_target_pairs={{0,2},{1,3},{2,0},{3,1},{4,6},{5,7},{6,4},{7,5},{8,10},{9,11},{10,... | collective-permute-start | bytes 884744 | tf_op jit(solution)/shard_map/ppermute | solution.py:1156
  45.7 15.6 %collective-permute-start.12 = (bf16[1024,768]{1,0:T(8,128)(2,1)S(1)}, bf16[1024,768]{1,0:T(8,128)(2,1)S(1)}, u32[]{:S(2)}, u32[]{:S(2)}) collective-permute-start(bf16[1024,768]{1,0:T(8,128)(2,1)S(1)} %get-tuple-element.153.refs_0_.refs_1_), channel_id=1, source_target_pairs={{0,1},{1,0},{2,3},{3,2},{4,5},{5,4},{6,7},{7,6},{8,9},{9,8},{10,11... | collective-permute-start | bytes 4718600 | tf_op jit(solution)/shard_map/ppermute | solution.py:1156
  45.8 15.6 %collective-permute-start.13 = (bf16[4,72,768]{2,1,0:T(8,128)(2,1)S(1)}, bf16[4,72,768]{2,1,0:T(8,128)(2,1)S(1)}, u32[]{:S(2)}, u32[]{:S(2)}) collective-permute-start(bf16[4,72,768]{2,1,0:T(8,128)(2,1)S(1)} %get-tuple-element.154.refs_3_), channel_id=1, source_target_pairs={{0,4},{4,0},{8,12},{12,8},{16,20},{20,16},{24,28},{28,24},{1,5},{5... | collective-permute-start | bytes 1327112 | tf_op jit(solution)/shard_map/ppermute | solution.py:1156
  48.2 13.2 %collective-permute-start.15 = (bf16[2,96,768]{2,1,0:T(8,128)(2,1)S(1)}, bf16[2,96,768]{2,1,0:T(8,128)(2,1)S(1)}, u32[]{:S(2)}, u32[]{:S(2)}) collective-permute-start(bf16[2,96,768]{2,1,0:T(8,128)(2,1)S(1)} %get-tuple-element.156.refs_7_), channel_id=1, source_target_pairs={{0,8},{4,12},{8,0},{12,4},{16,24},{20,28},{24,16},{28,20},{1,9},{5... | collective-permute-start | bytes 884744 | tf_op jit(solution)/shard_map/ppermute | solution.py:1156
  49.9 28.4 %collective-permute-start.18 = (bf16[4,48,1536]{2,1,0:T(8,128)(2,1)S(1)}, bf16[4,48,1536]{2,1,0:T(8,128)(2,1)S(1)}, u32[]{:S(2)}, u32[]{:S(2)}) collective-permute-start(bf16[4,48,1536]{2,1,0:T(8,128)(2,1)S(1)} %get-tuple-element.162.refs_4_), channel_id=1, source_target_pairs={{0,16},{4,20},{8,24},{12,28},{16,0},{20,4},{24,8},{28,12},{1,17},{... | collective-permute-start | bytes 1769480 | tf_op jit(solution)/shard_map/ppermute | solution.py:1156
  64.4 13.9 %collective-permute-start.16 = (bf16[4,48,768]{2,1,0:T(8,128)(2,1)S(1)}, bf16[4,48,768]{2,1,0:T(8,128)(2,1)S(1)}, u32[]{:S(2)}, u32[]{:S(2)}) collective-permute-start(bf16[4,48,768]{2,1,0:T(8,128)(2,1)S(1)} %get-tuple-element.160.refs_0_), channel_id=1, source_target_pairs={{0,4},{4,0},{8,12},{12,8},{16,20},{20,16},{24,28},{28,24},{1,5},{5... | collective-permute-start | bytes 884744 | tf_op jit(solution)/shard_map/ppermute | solution.py:1156
  64.9 13.4 %collective-permute-start.17 = (bf16[4,48,768]{2,1,0:T(8,128)(2,1)S(1)}, bf16[4,48,768]{2,1,0:T(8,128)(2,1)S(1)}, u32[]{:S(2)}, u32[]{:S(2)}) collective-permute-start(bf16[4,48,768]{2,1,0:T(8,128)(2,1)S(1)} %get-tuple-element.161.refs_2_), channel_id=1, source_target_pairs={{0,2},{1,3},{2,0},{3,1},{4,6},{5,7},{6,4},{7,5},{8,10},{9,11},{10,... | collective-permute-start | bytes 884744 | tf_op jit(solution)/shard_map/ppermute | solution.py:1156
  65.8 13.3 %collective-permute-start.19 = (bf16[8,48,384]{2,1,0:T(8,128)(2,1)S(1)}, bf16[8,48,384]{2,1,0:T(8,128)(2,1)S(1)}, u32[]{:S(2)}, u32[]{:S(2)}) collective-permute-start(bf16[8,48,384]{2,1,0:T(8,128)(2,1)S(1)} %get-tuple-element.163.refs_6_), channel_id=1, source_target_pairs={{0,4},{4,0},{8,12},{12,8},{16,20},{20,16},{24,28},{28,24},{1,5},{5... | collective-permute-start | bytes 884744 | tf_op jit(solution)/shard_map/ppermute | solution.py:1156
  79.3 22.1 %collective-permute-start.21 = (bf16[8,48,768]{2,1,0:T(8,128)(2,1)S(1)}, bf16[8,48,768]{2,1,0:T(8,128)(2,1)S(1)}, u32[]{:S(2)}, u32[]{:S(2)}) collective-permute-start(bf16[8,48,768]{2,1,0:T(8,128)(2,1)S(1)} %get-tuple-element.168.refs_7_), channel_id=1, source_target_pairs={{0,2},{1,3},{2,0},{3,1},{4,6},{5,7},{6,4},{7,5},{8,10},{9,11},{10,... | collective-permute-start | bytes 1769480 | tf_op jit(solution)/shard_map/ppermute | solution.py:1156
  80.3 21.1 %collective-permute-start.22 = (bf16[8,48,768]{2,1,0:T(8,128)(2,1)S(1)}, bf16[8,48,768]{2,1,0:T(8,128)(2,1)S(1)}, u32[]{:S(2)}, u32[]{:S(2)}) collective-permute-start(bf16[8,48,768]{2,1,0:T(8,128)(2,1)S(1)} %get-tuple-element.169.refs_9_), channel_id=1, source_target_pairs={{0,4},{4,0},{8,12},{12,8},{16,20},{20,16},{24,28},{28,24},{1,5},{5... | collective-permute-start | bytes 1769480 | tf_op jit(solution)/shard_map/ppermute | solution.py:1156
  80.6 26.3 %collective-permute-start.25 = (bf16[8,48,1536]{2,1,0:T(8,128)(2,1)S(1)}, bf16[8,48,1536]{2,1,0:T(8,128)(2,1)S(1)}, u32[]{:S(2)}, u32[]{:S(2)}) collective-permute-start(bf16[8,48,1536]{2,1,0:T(8,128)(2,1)S(1)} %get-tuple-element.164.refs_4_), channel_id=1, source_target_pairs={{0,8},{4,12},{8,0},{12,4},{16,24},{20,28},{24,16},{28,20},{1,9},{5... | collective-permute-start | bytes 3538952 | tf_op jit(solution)/shard_map/ppermute | solution.py:1156
  134.5 28.3 %collective-permute-start.33 = (bf16[8,96,768]{2,1,0:T(8,128)(2,1)S(1)}, bf16[8,96,768]{2,1,0:T(8,128)(2,1)S(1)}, u32[]{:S(2)}, u32[]{:S(2)}) collective-permute-start(bf16[8,96,768]{2,1,0:T(8,128)(2,1)S(1)} %get-tuple-element.198), channel_id=1, source_target_pairs={{0,4},{4,0},{8,12},{12,8},{16,20},{20,16},{24,28},{28,24},{1,5},{5... | collective-permute-start | bytes 3538952 | tf_op jit(solution)/shard_map/ppermute | solution.py:1156
  136.1 28.0 %collective-permute-start.34 = (bf16[8,48,1536]{2,1,0:T(8,128)(2,1)S(1)}, bf16[8,48,1536]{2,1,0:T(8,128)(2,1)S(1)}, u32[]{:S(2)}, u32[]{:S(2)}) collective-permute-start(bf16[8,48,1536]{2,1,0:T(8,128)(2,1)S(1)} %get-tuple-element.199), channel_id=1, source_target_pairs={{0,8},{4,12},{8,0},{12,4},{16,24},{20,28},{24,16},{28,20},{1,9},{5... | collective-permute-start | bytes 3538952 | tf_op jit(solution)/shard_map/ppermute | solution.py:1156
  137.5 12.1 %collective-permute-start.32 = (bf16[192,1024]{1,0:T(8,128)(2,1)S(1)}, bf16[192,1024]{1,0:T(8,128)(2,1)S(1)}, u32[]{:S(2)}, u32[]{:S(2)}) collective-permute-start(bf16[192,1024]{1,0:T(8,128)(2,1)S(1)} %get-tuple-element.192.refs_4_), channel_id=1, source_target_pairs={{0,2},{1,3},{2,0},{3,1},{4,6},{5,7},{6,4},{7,5},{8,10},{9,11},{10,... | collective-permute-start | bytes 1179656 | tf_op jit(solution)/shard_map/ppermute | solution.py:1156
  139.6 24.5 %collective-permute-start.35 = (bf16[8,48,384]{2,1,0:T(8,128)(2,1)S(1)}, bf16[8,48,384]{2,1,0:T(8,128)(2,1)S(1)}, u32[]{:S(2)}, u32[]{:S(2)}) collective-permute-start(bf16[8,48,384]{2,1,0:T(8,128)(2,1)S(1)} %get-tuple-element.200), channel_id=1, source_target_pairs={{0,2},{1,3},{2,0},{3,1},{4,6},{5,7},{6,4},{7,5},{8,10},{9,11},{10,... | collective-permute-start | bytes 884744 | tf_op jit(solution)/shard_map/ppermute | solution.py:1156
  164.9 21.4 %collective-permute-start.36 = (bf16[4,96,768]{2,1,0:T(8,128)(2,1)S(1)}, bf16[4,96,768]{2,1,0:T(8,128)(2,1)S(1)}, u32[]{:S(2)}, u32[]{:S(2)}) collective-permute-start(bf16[4,96,768]{2,1,0:T(8,128)(2,1)S(1)} %get-tuple-element.205), channel_id=1, source_target_pairs={{0,8},{4,12},{8,0},{12,4},{16,24},{20,28},{24,16},{28,20},{1,9},{5... | collective-permute-start | bytes 1769480 | tf_op jit(solution)/shard_map/ppermute | solution.py:1156
  165.2 21.1 %collective-permute-start.37 = (bf16[4,48,1536]{2,1,0:T(8,128)(2,1)S(1)}, bf16[4,48,1536]{2,1,0:T(8,128)(2,1)S(1)}, u32[]{:S(2)}, u32[]{:S(2)}) collective-permute-start(bf16[4,48,1536]{2,1,0:T(8,128)(2,1)S(1)} %get-tuple-element.206), channel_id=1, source_target_pairs={{0,2},{1,3},{2,0},{3,1},{4,6},{5,7},{6,4},{7,5},{8,10},{9,11},{10,... | collective-permute-start | bytes 1769480 | tf_op jit(solution)/shard_map/ppermute | solution.py:1156
  165.9 20.4 %collective-permute-start.38 = (bf16[4,48,384]{2,1,0:T(8,128)(2,1)S(1)}, bf16[4,48,384]{2,1,0:T(8,128)(2,1)S(1)}, u32[]{:S(2)}, u32[]{:S(2)}) collective-permute-start(bf16[4,48,384]{2,1,0:T(8,128)(2,1)S(1)} %get-tuple-element.208), channel_id=1, source_target_pairs={{0,8},{4,12},{8,0},{12,4},{16,24},{20,28},{24,16},{28,20},{1,9},{5... | collective-permute-start | bytes 442376 | tf_op jit(solution)/shard_map/ppermute | solution.py:1156
  190.6 12.7 %collective-permute-start.41 = (bf16[12,24,768]{2,1,0:T(8,128)(2,1)}, bf16[12,24,768]{2,1,0:T(8,128)(2,1)}, u32[]{:S(2)}, u32[]{:S(2)}) collective-permute-start(bf16[12,24,768]{2,1,0:T(8,128)(2,1)} %get-tuple-element.215), channel_id=1, source_target_pairs={{0,8},{4,12},{8,0},{12,4},{16,24},{20,28},{24,16},{28,20},{1,9},{5... | collective-permute-start | bytes 1327112 | tf_op jit(solution)/shard_map/ppermute | solution.py:1156
  194.4 13.3 %collective-permute-start.39 = (bf16[256,768]{1,0:T(8,128)(2,1)}, bf16[256,768]{1,0:T(8,128)(2,1)}, u32[]{:S(2)}, u32[]{:S(2)}) collective-permute-start(bf16[256,768]{1,0:T(8,128)(2,1)} %get-tuple-element.212), channel_id=1, source_target_pairs={{0,1},{1,0},{2,3},{3,2},{4,5},{5,4},{6,7},{7,6},{8,9},{9,8},{10,11... | collective-permute-start | bytes 1179656 | tf_op jit(solution)/shard_map/ppermute | solution.py:1156
  194.4 13.3 %collective-permute-start.40 = (bf16[256,768]{1,0:T(8,128)(2,1)}, bf16[256,768]{1,0:T(8,128)(2,1)}, u32[]{:S(2)}, u32[]{:S(2)}) collective-permute-start(bf16[256,768]{1,0:T(8,128)(2,1)} %get-tuple-element.213), channel_id=1, source_target_pairs={{0,1},{1,0},{2,3},{3,2},{4,5},{5,4},{6,7},{7,6},{8,9},{9,8},{10,11... | collective-permute-start | bytes 1179656 | tf_op jit(solution)/shard_map/ppermute | solution.py:1156
  200.3 15.4 %collective-permute-start.48 = (bf16[1,48,1920]{2,1,0:T(8,128)(2,1)}, bf16[1,48,1920]{2,1,0:T(8,128)(2,1)}, u32[]{:S(2)}, u32[]{:S(2)}) collective-permute-start(bf16[1,48,1920]{2,1,0:T(8,128)(2,1)} %get-tuple-element.228), channel_id=1, source_target_pairs={{0,16},{4,20},{8,24},{12,28},{16,0},{20,4},{24,8},{28,12},{1,17},{... | collective-permute-start | bytes 552968 | tf_op jit(solution)/shard_map/ppermute | solution.py:1156
  203.2 12.4 %collective-permute-start.47 = (bf16[1,96,768]{2,1,0:T(8,128)(2,1)}, bf16[1,96,768]{2,1,0:T(8,128)(2,1)}, u32[]{:S(2)}, u32[]{:S(2)}) collective-permute-start(bf16[1,96,768]{2,1,0:T(8,128)(2,1)} %get-tuple-element.226), channel_id=1, source_target_pairs={{0,16},{4,20},{8,24},{12,28},{16,0},{20,4},{24,8},{28,12},{1,17},{... | collective-permute-start | bytes 442376 | tf_op jit(solution)/shard_map/ppermute | solution.py:1156
  206.4 12.3 %collective-permute-start.46 = (bf16[6,24,768]{2,1,0:T(8,128)(2,1)}, bf16[6,24,768]{2,1,0:T(8,128)(2,1)}, u32[]{:S(2)}, u32[]{:S(2)}) collective-permute-start(bf16[6,24,768]{2,1,0:T(8,128)(2,1)} %get-tuple-element.225), channel_id=1, source_target_pairs={{0,4},{4,0},{8,12},{12,8},{16,20},{20,16},{24,28},{28,24},{1,5},{5... | collective-permute-start | bytes 663560 | tf_op jit(solution)/shard_map/ppermute | solution.py:1156
  212.8 16.2 %collective-permute-start.45 = (bf16[512,768]{1,0:T(8,128)(2,1)}, bf16[512,768]{1,0:T(8,128)(2,1)S(1)}, u32[]{:S(2)}, u32[]{:S(2)}) collective-permute-start(bf16[512,768]{1,0:T(8,128)(2,1)} %get-tuple-element.222.refs_4_), channel_id=1, source_target_pairs={{0,2},{1,3},{2,0},{3,1},{4,6},{5,7},{6,4},{7,5},{8,10},{9,11},{10,... | collective-permute-start | bytes 2359304 | tf_op jit(solution)/shard_map/ppermute | solution.py:1156
  214.3 23.3 %collective-permute-start.44 = (bf16[512,768]{1,0:T(8,128)(2,1)}, bf16[512,768]{1,0:T(8,128)(2,1)}, u32[]{:S(2)}, u32[]{:S(2)}) collective-permute-start(bf16[512,768]{1,0:T(8,128)(2,1)} %get-tuple-element.221), channel_id=1, source_target_pairs={{0,1},{1,0},{2,3},{3,2},{4,5},{5,4},{6,7},{7,6},{8,9},{9,8},{10,11... | collective-permute-start | bytes 2359304 | tf_op jit(solution)/shard_map/ppermute | solution.py:1156
  229.0 13.2 %collective-permute-start.50 = (f32[24,768]{1,0:T(8,128)S(1)}, f32[24,768]{1,0:T(8,128)S(1)}, u32[]{:S(2)}, u32[]{:S(2)}) collective-permute-start(f32[24,768]{1,0:T(8,128)S(1)} %get-tuple-element.267), channel_id=1, source_target_pairs={{0,0},{12,1},{24,2},{5,3},{17,4},{29,5},{10,6},{22,7},{3,8},{15,9}... | collective-permute-start | bytes 221192 | tf_op jit(solution)/shard_map/ppermute | solution.py:1344
  229.7 12.6 %collective-permute-start.51 = (f32[24,768]{1,0:T(8,128)S(1)}, f32[24,768]{1,0:T(8,128)S(1)}, u32[]{:S(2)}, u32[]{:S(2)}) collective-permute-start(f32[24,768]{1,0:T(8,128)S(1)} %get-tuple-element.266), channel_id=1, source_target_pairs={{4,0},{16,1},{28,2},{9,3},{21,4},{2,5},{14,6},{26,7},{7,8},{19,9},... | collective-permute-start | bytes 221192 | tf_op jit(solution)/shard_map/ppermute | solution.py:1344
  (83 other events, 835.3 us)
